TPU v7x, 128 devices: a whole 4x4x4 slice. The times are simulated.
128 devices in a mesh: tm: 8 (over z_hi, x), space: 16 (over y, z_lo, core).
Axes of the slice: x: 4, y: 4, z: 4 (z_hi: 2, z_lo: 2; z = z_hi * 2 + z_lo), core: 2. Of those that a mesh axis runs over, the one named last changes fastest.
Arguments:
- courant: float32 [64, 256, 256], P('space'), may hold values from 0.04 to 0.3
- misfit: float32 [64, 256, 256], P('space'), may hold values from -6 to 6
- wavelet: float32 [128], P('tm'), may hold values from -1.5 to 1.5
- source_cells: int32 [128], P('tm'), may hold values from 0 to 4194303
- boundary_states: float32 [8, 2, 64, 256, 256], P('tm', None, 'space'), may hold values from -6 to 6
Outputs:
- updated_states: float32 [8, 2, 64, 256, 256], P('tm', None, 'space')
- source_gradient: float32 [128], P('tm')
Inputs may be any that keep to these rules, and one draw needn't show every extreme that they name: `source_cells`: each entry is a flattened cell index x * 256 * 256 + y * 256 + z of the fine grid.
All inputs are finite; a program needn't handle non-finite values.
Results may differ from a plain program's by a relative error of at most 0.0001.
Values sent between devices are 32-bit elements; how exact they have to be, the bound alone decides.
No kernel may reach another device: no remote copies, remote signals or barrier semaphores. Data moves between devices by JAX's collectives and lax.ppermute only.
A program may use at most 192 MiB of HBM per device.

v0:
```python
import functools

import jax
import jax.numpy as jnp
from jax import lax
from jax.experimental import pallas as pl
from jax.experimental.pallas import tpu as pltpu
from jax.sharding import PartitionSpec as P

COARSE = 8
GROUPS = 8
SLABS = 16
ROWS = 32
UNROLL = 8
HIGH = lax.Precision.HIGHEST

SNAKE = tuple(
    y * 4 + z * 2 + c for y in range(4) for z in ((0, 1) if y % 2 == 0 else (1, 0)) for c in (0, 1)
)
PLACE = tuple(SNAKE.index(s) for s in range(SLABS))
VM = pl.BlockSpec(memory_space=pltpu.VMEM)
SM = pl.BlockSpec(memory_space=pltpu.SMEM)
HB = pl.BlockSpec(memory_space=pltpu.HBM)


def exchange(block, order, offset):
    pairs = []
    for row in range(GROUPS):
        base, beside = row * SLABS, (row ^ 1) * SLABS
        for i in range(offset, SLABS - 1, 2):
            here, there = base + order[i], base + order[i + 1]
            pairs += [(here, there), (there, here)]
        if offset:
            pairs += [(base + end, beside + end) for end in (order[0], order[-1])]
    return lax.ppermute(block, ("tm", "space"), pairs)


def call(kernel, out_shapes, args, specs, scratch=(), aliases=None, cost=None):
    return pl.pallas_call(
        kernel,
        out_shape=out_shapes,
        in_specs=specs,
        out_specs=jax.tree.map(lambda _: VM, out_shapes),
        scratch_shapes=list(scratch),
        input_output_aliases=aliases or {},
        cost_estimate=cost,
        compiler_params=pltpu.CompilerParams(vmem_limit_bytes=16 << 20),
    )(*args)


def f32(*shape):
    return jax.ShapeDtypeStruct(shape, jnp.float32)


def halving(rows, cols):
    r = lax.broadcasted_iota(jnp.int32, (rows, cols), 0)
    c = lax.broadcasted_iota(jnp.int32, (rows, cols), 1)
    hit = c // 2 == r if rows < cols else r // 2 == c
    return jnp.where(hit, 1.0, 0.0).astype(jnp.bfloat16)


def dot(a, ones):
    total = None
    for _ in range(3):
        part = a.astype(jnp.bfloat16)
        a = a - part.astype(jnp.float32)
        term = jnp.dot(part, ones, preferred_element_type=jnp.float32)
        total = term if total is None else total + term
    return total


def restrict_planes(first, second, tall):
    ny, nz = first.shape
    tall[...] = dot(first[...] + second[...], halving(nz, nz // 2))
    half = ny // 2
    return (tall[pl.ds(0, half, stride=2), :] + tall[pl.ds(1, half, stride=2), :]) * 0.125


def update_plane(mid, lower, upper, before, speed, force, weight, out, reach=None):
    ny, nz = mid.shape
    lane = lax.broadcasted_iota(jnp.int32, (ROWS, nz), 1)
    row = lax.broadcasted_iota(jnp.int32, (ROWS, nz), 0)
    for r0 in range(0, ny, ROWS):
        here = slice(r0, r0 + ROWS)
        m = mid[here, :]
        if r0 == 0:
            up = jnp.where(row == 0, 0.0, pltpu.roll(m, 1, 0))
        else:
            up = mid[r0 - 1 : r0 - 1 + ROWS, :]
        if r0 + ROWS == ny:
            down = jnp.where(row == ROWS - 1, 0.0, pltpu.roll(m, ROWS - 1, 0))
        else:
            down = mid[r0 + 1 : r0 + 1 + ROWS, :]
        left = jnp.where(lane == 0, 0.0, pltpu.roll(m, 1, 1))
        right = jnp.where(lane == nz - 1, 0.0, pltpu.roll(m, nz - 1, 1))
        low = lower[here, :] if reach is None else lower[here, :] * reach
        if upper is not None:
            low = low + upper[here, :]
        beside = low + (up + down) + (left + right)
        out[here, :] = (
            2.0 * m - before[here, :] + speed[here, :] * (beside - 6.0 * m) + weight * force[here, :]
        )


def sampled_row(planes, info, cell):
    ny, nz = planes[0].shape
    x = cell // (ny * nz) - info[1] * len(planes)
    y = lax.rem(cell // nz, ny)
    z = lax.rem(cell, nz)
    q = jnp.where(info[0] == 1, len(planes) - 1 - x, x)
    lane = lax.broadcasted_iota(jnp.int32, (1, nz), 1)
    row = jnp.zeros((1, nz), jnp.float32)
    for k, plane in enumerate(planes):
        row = jnp.where((lane == z) & (q == k), plane[pl.ds(y, 1), :], row)
    return row


def prep_kernel(info, courant, misfit, states, ce, ci, fe, fi, e0, inner, b0, binner, sems):
    def spread(flip):
        q = (lambda k: 3 - k) if flip else (lambda k: k)
        moves = [(states.at[0, q(0)], e0), (courant.at[q(0)], ce), (misfit.at[q(0)], fe)]
        moves += [(states.at[1, q(0)], b0)]
        for k in range(3):
            moves += [(states.at[0, q(k + 1)], inner.at[k]), (states.at[1, q(k + 1)], binner.at[k])]
            moves += [(courant.at[q(k + 1)], ci.at[k]), (misfit.at[q(k + 1)], fi.at[k])]
        copies = [pltpu.make_async_copy(a, b, sems.at[i]) for i, (a, b) in enumerate(moves)]
        for copy in copies:
            copy.start()
        for copy in copies:
            copy.wait()

    @pl.when(info[0] == 1)
    def _():
        spread(True)

    @pl.when(info[0] == 0)
    def _():
        spread(False)

    @pl.when(info[2] == 0)
    def _():
        for ref in (e0, inner, b0, binner):
            ref[...] = jnp.zeros_like(ref)


def restrict_kernel(courant, states, rb, rc, tall):
    block = rc.shape[2]
    for xc in range(2):
        r = restrict_planes(courant.at[2 * xc], courant.at[2 * xc + 1], tall)
        for s in range(SLABS):
            rc[s, xc] = r[PLACE[s] * block : (PLACE[s] + 1) * block, :]
        for lev in range(2):
            rb[lev, xc] = restrict_planes(states.at[lev, 2 * xc], states.at[lev, 2 * xc + 1], tall)


def edge_kernel(level, weights, reach, e0, inner, b0, off, ce, fe, n0):
    weight = weights[level : level + 1, :]
    update_plane(e0, off, inner.at[0], b0, ce, fe, weight, n0, reach[...])


def inner_kernel(level, taken, info, cells, weights, e0, inner, before, on, ci, fi, samples, n1, out, out_samples, beside):
    weight = weights[level : level + 1, :]
    ny = e0.shape[0]

    def pair(k, carry):
        here = pl.ds(pl.multiple_of(k * ROWS, ROWS), ROWS)
        beside[0, here, :] = e0[here, :] + inner[1, here, :]
        beside[1, here, :] = inner[0, here, :] + inner[2, here, :]
        beside[2, here, :] = inner[1, here, :] + on[here, :]
        return carry

    lax.fori_loop(0, ny // ROWS, pair, 0)

    def plane(k, carry):
        update_plane(inner.at[k], beside.at[k], None, before.at[k], ci.at[k], fi.at[k], weight, out.at[k])
        return carry

    lax.fori_loop(0, 3, plane, 0)

    def copy(k, carry):
        here = pl.ds(pl.multiple_of(k * ROWS, ROWS), ROWS)
        n1[here, :] = out[2, here, :]
        return carry

    lax.fori_loop(0, ny // ROWS, copy, 0)
    out_samples[...] = samples[...]
    if taken is not None:
        planes = (e0, inner.at[0], inner.at[1], inner.at[2])
        out_samples[taken : taken + 1, :] = sampled_row(planes, info, cells[taken])


def leave_kernel(info, cells, e0, inner, b0, binner, samples, rb, rc, out, sums, tall):
    odd = info[0] == 1
    block = out.shape[2]
    for lev, (first, mid) in enumerate(((e0, inner), (b0, binner))):
        sums[0] = restrict_planes(first, mid.at[0], tall)
        sums[1] = restrict_planes(mid.at[1], mid.at[2], tall)
        for xc in range(2):
            r = jnp.where(odd, sums[1 - xc], sums[xc]) - rb[lev, xc]
            for s in range(SLABS):
                out[s, lev * 2 + xc] = r[PLACE[s] * block : (PLACE[s] + 1) * block, :]
    for s in range(SLABS):
        out[s, 5:7] = rc[s]
    row = sampled_row((e0, inner.at[0], inner.at[1], inner.at[2]), info, cells[0])
    count = samples.shape[0]
    at = lax.broadcasted_iota(jnp.int32, (count, 1), 0)
    values = jnp.where(at == 0, jnp.sum(row), jnp.sum(samples[...], axis=1, keepdims=True))
    lane = lax.broadcasted_iota(jnp.int32, (count, 128), 1)
    level = lax.broadcasted_iota(jnp.int32, (count, 128), 0)
    line = jnp.sum(jnp.where(lane == level, values, 0.0), axis=0, keepdims=True)
    for s in range(SLABS):
        out[s, 4] = jnp.broadcast_to(line, (block, 128))


def phi_kernel(has_add, flags, state, on, off, speed, son, soff, *rest):
    if has_add:
        add, out, a, b, c = rest
    else:
        out, a, b, c = rest
    odd = flags[0:1, :] > 0.5
    near = flags[1:2, :]
    nx = speed.shape[0] * speed.shape[1]
    block = speed.shape[2]
    tall, nz = 3 * block, 128
    zero = jnp.zeros((tall, nz), jnp.float32)
    a[0], a[nx + 1], b[0], b[nx + 1] = zero, zero, zero, zero

    def fill(target, mine, other, far):
        far = far.reshape(nx, block, nz) * near
        other = other.reshape(nx, block, nz)
        target(slice(0, block), jnp.where(odd, other, far))
        target(slice(block, 2 * block), mine.reshape(nx, block, nz))
        target(slice(2 * block, tall), jnp.where(odd, far, other))

    def to_a(rows, value):
        a[1 : nx + 1, rows, :] = value

    def to_b(rows, value):
        b[1 : nx + 1, rows, :] = value

    def to_c(rows, value):
        c[:, rows, :] = value

    fill(to_a, state[:, 0:2], on[:, 0:2], off[:, 0:2])
    fill(to_b, state[:, 2:4], on[:, 2:4], off[:, 2:4])
    fill(to_c, speed[...], son[...], soff[...])

    step_x = 4
    lane = lax.broadcasted_iota(jnp.int32, (step_x, tall, nz), 2)

    def turn(now, then):
        def some(k, carry):
            x0 = k * step_x
            m = now[pl.ds(x0 + 1, step_x)]
            beside = now[pl.ds(x0, step_x)] + now[pl.ds(x0 + 2, step_x)]
            beside = beside + pltpu.roll(m, 1, 1) + pltpu.roll(m, tall - 1, 1)
            beside = beside + jnp.where(lane == 0, 0.0, pltpu.roll(m, 1, 2))
            beside = beside + jnp.where(lane == nz - 1, 0.0, pltpu.roll(m, nz - 1, 2))
            then[pl.ds(x0 + 1, step_x)] = (
                2.0 * m - then[pl.ds(x0 + 1, step_x)] + c[pl.ds(x0, step_x)] * (beside - 6.0 * m)
            )
            return carry

        lax.fori_loop(0, nx // step_x, some, 0, unroll=UNROLL)

    def two(_, carry):
        turn(a, b)
        turn(b, a)
        return carry

    lax.fori_loop(0, COARSE // 2, two, 0)
    rows = slice(block, 2 * block)
    one = a[1 : nx + 1, rows, :].reshape(SLABS, 2, block, nz)
    other = b[1 : nx + 1, rows, :].reshape(SLABS, 2, block, nz)
    if has_add:
        one = one + add[:, 0:2]
        other = other + add[:, 2:4]
    out[:, 0:2] = one
    out[:, 2:4] = other


def arrive_kernel(coarse, states, out, tall):
    block = coarse.shape[2]
    nzc = tall.shape[1]
    for lev in range(2):
        for xc in range(2):
            for s in range(SLABS):
                piece = coarse[s, lev * 2 + xc]
                for row in (0, 1):
                    tall[pl.ds(2 * PLACE[s] * block + row, block, stride=2), :] = piece
            fine = dot(tall[...], halving(nzc, 2 * nzc))
            out[lev, 2 * xc] = states[lev, 2 * xc] + fine
            out[lev, 2 * xc + 1] = states[lev, 2 * xc + 1] + fine


def body(courant, misfit, wavelet, source_cells, boundary_states):
    steps = wavelet.shape[0]
    ny, nz = courant.shape[1:]
    nyc, nzc = ny // 2, nz // 2
    block = nyc // SLABS
    slab = lax.axis_index("space")
    tm = lax.axis_index("tm")
    states = boundary_states[0]
    natural = tuple(range(SLABS))
    odd = lax.rem(slab, 2)
    alive = (tm > 0).astype(jnp.int32)
    reach = ((slab > 0) & (slab < SLABS - 1)).astype(jnp.int32)
    creach = ((slab != SNAKE[0]) & (slab != SNAKE[-1])).astype(jnp.int32)
    info = jnp.stack([odd, slab, alive, reach, creach]).astype(jnp.int32)
    ring = [(i, (i + 1) % GROUPS) for i in range(GROUPS)]
    back = [(i, (i - 1) % GROUPS) for i in range(GROUPS)]

    mask = alive.astype(jnp.float32)
    first_off = lax.dynamic_index_in_dim(states[0], 3 * odd, 0, keepdims=False) * mask
    first_on = lax.dynamic_index_in_dim(states[0], 3 - 3 * odd, 0, keepdims=False) * mask
    off = exchange(first_off, natural, 1)
    on = exchange(first_on, natural, 0)
    wave, marks, _ = lax.optimization_barrier((wavelet, source_cells, first_off))
    packed = lax.ppermute(jnp.stack([wave, marks.astype(jnp.float32)]), "tm", ring)
    weights = jnp.broadcast_to(packed[0][:, None], (steps, nz))
    cells = packed[1].astype(jnp.int32)

    plane = f32(ny, nz)
    ce, ci, fe, fi, e0, inner, b0, binner = call(
        prep_kernel,
        (plane, f32(3, ny, nz)) * 4,
        (info, courant, misfit, states),
        [SM, HB, HB, HB],
        scratch=[pltpu.SemaphoreType.DMA((16,))],
    )
    away = jnp.broadcast_to(reach.astype(jnp.float32), (1, nz))
    samples = jnp.zeros((steps, nz), jnp.float32)
    for turn in range(steps):
        level = steps - 1 - turn
        n0 = call(
            functools.partial(edge_kernel, level),
            plane,
            (weights, away, e0, inner, b0, off, ce, fe),
            [VM] * 8,
        )
        if turn < steps - 1:
            off = exchange(n0, natural, 1)
        n1, ninner, samples = call(
            functools.partial(inner_kernel, level, level + 1 if turn else None),
            (plane, f32(3, ny, nz), f32(steps, nz)),
            (info, cells, weights, e0, inner, binner, on, ci, fi, samples),
            [SM, SM] + [VM] * 8,
            scratch=[pltpu.VMEM((3, ny, nz), jnp.float32)],
        )
        if turn == 2:
            gate = lax.optimization_barrier((courant, states, n0))
            rb, speed = call(
                restrict_kernel,
                (f32(2, 2, nyc, nzc), f32(SLABS, 2, block, nzc)),
                gate[:2],
                [VM, VM],
                scratch=[pltpu.VMEM((ny, nzc), jnp.float32)],
            )
            n1, rb, speed = lax.optimization_barrier((n1, rb, speed))
            rb = lax.ppermute(rb, "tm", ring)
        if turn == 8:
            n1, rb = lax.optimization_barrier((n1, rb))
        if turn < steps - 1:
            on = exchange(n1, natural, 0)
        e0, inner, b0, binner = n0, ninner, e0, inner

    pieces = call(
        leave_kernel,
        f32(SLABS, 7, block, nzc),
        (info, cells, e0, inner, b0, binner, samples, rb, speed),
        [SM, SM] + [VM] * 7,
        scratch=[pltpu.VMEM((2, nyc, nzc), jnp.float32), pltpu.VMEM((ny, nzc), jnp.float32)],
    )
    pieces = lax.all_to_all(pieces, "space", 0, 0)
    pieces, speed = pieces[:, :5], pieces[:, 5:7]
    lane = (1, nzc)
    parity = jnp.broadcast_to(odd.astype(jnp.float32), lane)
    near = jnp.broadcast_to(creach.astype(jnp.float32), lane)

    flags = jnp.concatenate([parity, near], axis=0)

    def phi(state, add=None):
        sides = (exchange(state, SNAKE, 1), exchange(state, SNAKE, 0))
        nx = SLABS * 2
        args = (flags, state, sides[1], sides[0], speed, son, soff)
        args = args + (() if add is None else (add,))
        return call(
            functools.partial(phi_kernel, add is not None),
            f32(SLABS, 4, block, nzc),
            args,
            [VM] * len(args),
            scratch=[pltpu.VMEM((nx + 2, 3 * block, nzc), jnp.float32)] * 2
            + [pltpu.VMEM((nx, 3 * block, nzc), jnp.float32)],
        )

    def later(state, distance, aligned):
        route = []
        for to in range(GROUPS):
            group = to if aligned else (to - 1) % GROUPS
            route.append(((group + distance + 1) % GROUPS, to))
        group = tm if aligned else lax.rem(tm + GROUPS - 1, GROUPS)
        return lax.ppermute(state, "tm", route) * (group + distance < GROUPS).astype(jnp.float32)

    soff = exchange(speed, SNAKE, 1)
    son = exchange(speed, SNAKE, 0)
    moved = lax.ppermute(pieces, "tm", back)
    moved, son, soff = lax.optimization_barrier((moved, son, soff))
    gradient = jnp.sum(moved[:, 4, 0, :steps], axis=0)
    moved = moved[:, :4] * (lax.rem(tm + GROUPS - 1, GROUPS) + 1 < GROUPS).astype(jnp.float32)
    total = phi(moved, pieces)
    moved = later(total, 2, False)
    total = phi(phi(moved), total)
    moved = later(total, 4, True)
    own = lax.ppermute(total, "tm", back)
    for turn in range(4):
        moved = phi(moved, own if turn == 3 else None)
        if turn == 1:
            moved, own = lax.optimization_barrier((moved, own))
    coarse = lax.all_to_all(moved, "space", 0, 0)
    updated = call(
        arrive_kernel,
        f32(2, 4, ny, nz),
        (coarse, states),
        [VM, VM],
        scratch=[pltpu.VMEM((ny, nzc), jnp.float32)],
    )
    return (updated[None], gradient)


def solution(mesh):
    placed = (
        P("space", None, None),
        P("space", None, None),
        P("tm"),
        P("tm"),
        P("tm", None, "space", None, None),
    )
    return jax.shard_map(
        body,
        mesh=mesh,
        in_specs=placed,
        out_specs=(P("tm", None, "space", None, None), P("tm")),
        check_vma=False,
    )
```

profile of v0, /device:TPU:7, one launch (start us, length us, event | category | flops | bytes accessed | tf_op | source)
XLA Modules:
  0.0 262.9 jit_solution(4499678546984505611)
XLA Ops:
  4.8 3.3 %collective-permute-start = (f32[2,16]{1,0:T(2,128)S(1)}, f32[2,16]{1,0:T(2,128)S(1)}, u32[]{:S(2)}, u32[]{:S(2)}) collective-permute-start(f32[2,16]{1,0:T(2,128)S(1)} %pad_maximum_fusion), channel_id=1, source_target_pairs={{0,16},{16,32},{32,48},{48,64},{64,80},{80,96},{96,112},{112,0},{1... | collective-permute-start | bytes 392 | tf_op jit(solution)/shard_map/ppermute | solution.py:319
  15.7 4.5 %collective-permute-done.3.off = f32[256,256]{1,0:T(8,128)S(1)} collective-permute-done((f32[256,256]{1,0:T(8,128)S(1)}, f32[256,256]{1,0:T(8,128)S(1)}, u32[]{:S(2)}, u32[]{:S(2)}) %collective-permute-start.3) | collective-permute-done | bytes 262176 | tf_op jit(solution)/shard_map/ppermute | solution.py:35
  24.7 2.8 %collective-permute-done.5.off = f32[256,256]{1,0:T(8,128)S(1)} collective-permute-done((f32[256,256]{1,0:T(8,128)S(1)}, f32[256,256]{1,0:T(8,128)S(1)}, u32[]{:S(2)}, u32[]{:S(2)}) %collective-permute-start.5) | collective-permute-done | bytes 262176 | tf_op jit(solution)/shard_map/ppermute | solution.py:35
  39.1 2.7 %collective-permute-done.9.off = f32[256,256]{1,0:T(8,128)S(1)} collective-permute-done((f32[256,256]{1,0:T(8,128)S(1)}, f32[256,256]{1,0:T(8,128)S(1)}, u32[]{:S(2)}, u32[]{:S(2)}) %collective-permute-start.9) | collective-permute-done | bytes 262176 | tf_op jit(solution)/shard_map/ppermute | solution.py:35
  53.4 2.7 %collective-permute-done.13.off = f32[256,256]{1,0:T(8,128)S(1)} collective-permute-done((f32[256,256]{1,0:T(8,128)S(1)}, f32[256,256]{1,0:T(8,128)S(1)}, u32[]{:S(2)}, u32[]{:S(2)}) %collective-permute-start.13) | collective-permute-done | bytes 262176 | tf_op jit(solution)/shard_map/ppermute | solution.py:35
  67.8 3.6 %collective-permute-start.20 = (f32[2,2,128,128]{3,2,1,0:T(8,128)S(1)}, f32[2,2,128,128]{3,2,1,0:T(8,128)S(1)}, u32[]{:S(2)}, u32[]{:S(2)}) collective-permute-start(f32[2,2,128,128]{3,2,1,0:T(8,128)S(1)} %get-tuple-element.114), channel_id=1, source_target_pairs={{0,16},{16,32},{32,48},{48,64},{64,80},{80,96},{96,112},{112,0},{1... | collective-permute-start | bytes 786440 | tf_op jit(solution)/shard_map/ppermute | solution.py:360
  74.8 2.9 %collective-permute-done.20.rb = f32[2,2,128,128]{3,2,1,0:T(8,128)S(1)} collective-permute-done((f32[2,2,128,128]{3,2,1,0:T(8,128)S(1)}, f32[2,2,128,128]{3,2,1,0:T(8,128)S(1)}, u32[]{:S(2)}, u32[]{:S(2)}) %collective-permute-start.20) | collective-permute-done | bytes 262176 | tf_op jit(solution)/shard_map/ppermute | solution.py:360
  83.9 2.8 %collective-permute-done.22.off = f32[256,256]{1,0:T(8,128)S(1)} collective-permute-done((f32[256,256]{1,0:T(8,128)S(1)}, f32[256,256]{1,0:T(8,128)S(1)}, u32[]{:S(2)}, u32[]{:S(2)}) %collective-permute-start.22) | collective-permute-done | bytes 262176 | tf_op jit(solution)/shard_map/ppermute | solution.py:35
  126.3 16.9 %all_to_all.10 = f32[16,7,8,128]{3,2,1,0:T(8,128)S(1)} all-to-all(f32[16,7,8,128]{3,2,1,0:T(8,128)S(1)} %shard_map.102), channel_id=1, replica_groups=mesh['tm'=8,'space'=16] {'space'}, dimensions={0} | all-to-all | bytes 917504 | tf_op jit(solution)/shard_map/all_to_all | solution.py:374
  145.4 3.7 %collective-permute-done.36.soff = f32[16,2,8,128]{3,2,1,0:T(8,128)S(1)} collective-permute-done((f32[16,2,8,128]{3,2,1,0:T(8,128)S(1)}, f32[16,2,8,128]{3,2,1,0:T(8,128)S(1)}, u32[]{:S(2)}, u32[]{:S(2)}) %collective-permute-start.36) | collective-permute-done | bytes 131104 | tf_op jit(solution)/shard_map/ppermute | solution.py:35
  149.1 7.7 %collective-permute-done.34 = f32[16,5,8,128]{3,2,1,0:T(8,128)S(1)} collective-permute-done((f32[16,5,8,128]{3,2,1,0:T(8,128)S(1)}, f32[16,5,8,128]{3,2,1,0:T(8,128)S(1)}, u32[]{:S(2)}, u32[]{:S(2)}) %collective-permute-start.34) | collective-permute-done | bytes 327712 | tf_op jit(solution)/shard_map/ppermute | solution.py:406
  161.1 4.3 %collective-permute-done.38.off = f32[16,4,8,128]{3,2,1,0:T(8,128)} collective-permute-done((f32[16,4,8,128]{3,2,1,0:T(8,128)S(1)}, f32[16,4,8,128]{3,2,1,0:T(8,128)}, u32[]{:S(2)}, u32[]{:S(2)}) %collective-permute-start.38) | collective-permute-done | bytes 262176 | tf_op jit(solution)/shard_map/ppermute | solution.py:35
  166.4 3.0 %shard_map.103.rest_0_ = f32[16,4,8,128]{3,2,1,0:T(8,128)S(1)} custom-call(f32[2,128]{1,0:T(2,128)S(1)} %concatenate.6.flags, f32[16,4,8,128]{3,2,1,0:T(8,128)S(1)} %slice_multiply_fusion.state, f32[16,4,8,128]{3,2,1,0:T(8,128)S(1)} %copy-done.5, f32[16,4,8,128]{3,2,1,0:T(8,128)} %collective-permute-done.38.off, f32[16,2,8,128]{3,2,1,0:T(8,128)S(1)} %slice.31.speed, ...), custom_call_target="tpu_custom_call" | custom-call | tf_op jit(solution)/shard_map/pallas_call | solution.py:39
  169.6 11.4 %collective-permute-done.39 = f32[16,4,8,128]{3,2,1,0:T(8,128)S(1)} collective-permute-done((f32[16,4,8,128]{3,2,1,0:T(8,128)S(1)}, f32[16,4,8,128]{3,2,1,0:T(8,128)S(1)}, u32[]{:S(2)}, u32[]{:S(2)}) %collective-permute-start.39) | collective-permute-done | bytes 262176 | tf_op jit(solution)/shard_map/ppermute | solution.py:402
  183.4 4.9 %collective-permute-done.41.off = f32[16,4,8,128]{3,2,1,0:T(8,128)S(1)} collective-permute-done((f32[16,4,8,128]{3,2,1,0:T(8,128)S(1)}, f32[16,4,8,128]{3,2,1,0:T(8,128)S(1)}, u32[]{:S(2)}, u32[]{:S(2)}) %collective-permute-start.41) | collective-permute-done | bytes 262176 | tf_op jit(solution)/shard_map/ppermute | solution.py:35
  192.3 4.9 %collective-permute-done.43.off = f32[16,4,8,128]{3,2,1,0:T(8,128)S(1)} collective-permute-done((f32[16,4,8,128]{3,2,1,0:T(8,128)S(1)}, f32[16,4,8,128]{3,2,1,0:T(8,128)S(1)}, u32[]{:S(2)}, u32[]{:S(2)}) %collective-permute-start.43) | collective-permute-done | bytes 262176 | tf_op jit(solution)/shard_map/ppermute | solution.py:35
  199.4 8.7 %collective-permute-done.44 = f32[16,4,8,128]{3,2,1,0:T(8,128)S(1)} collective-permute-done((f32[16,4,8,128]{3,2,1,0:T(8,128)S(1)}, f32[16,4,8,128]{3,2,1,0:T(8,128)S(1)}, u32[]{:S(2)}, u32[]{:S(2)}) %collective-permute-start.44) | collective-permute-done | bytes 262176 | tf_op jit(solution)/shard_map/ppermute | solution.py:402
  210.6 4.9 %collective-permute-done.46.off = f32[16,4,8,128]{3,2,1,0:T(8,128)S(1)} collective-permute-done((f32[16,4,8,128]{3,2,1,0:T(8,128)S(1)}, f32[16,4,8,128]{3,2,1,0:T(8,128)S(1)}, u32[]{:S(2)}, u32[]{:S(2)}) %collective-permute-start.46) | collective-permute-done | bytes 262176 | tf_op jit(solution)/shard_map/ppermute | solution.py:35
  219.2 10.5 %collective-permute-done.48.off = f32[16,4,8,128]{3,2,1,0:T(8,128)S(1)} collective-permute-done((f32[16,4,8,128]{3,2,1,0:T(8,128)S(1)}, f32[16,4,8,128]{3,2,1,0:T(8,128)S(1)}, u32[]{:S(2)}, u32[]{:S(2)}) %collective-permute-start.48) | collective-permute-done | bytes 262176 | tf_op jit(solution)/shard_map/ppermute | solution.py:35
  233.4 4.6 %collective-permute-done.51.off = f32[16,4,8,128]{3,2,1,0:T(8,128)S(1)} collective-permute-done((f32[16,4,8,128]{3,2,1,0:T(8,128)S(1)}, f32[16,4,8,128]{3,2,1,0:T(8,128)S(1)}, u32[]{:S(2)}, u32[]{:S(2)}) %collective-permute-start.51) | collective-permute-done | bytes 262176 | tf_op jit(solution)/shard_map/ppermute | solution.py:35
  242.1 4.9 %collective-permute-done.53.off = f32[16,4,8,128]{3,2,1,0:T(8,128)S(1)} collective-permute-done((f32[16,4,8,128]{3,2,1,0:T(8,128)S(1)}, f32[16,4,8,128]{3,2,1,0:T(8,128)S(1)}, u32[]{:S(2)}, u32[]{:S(2)}) %collective-permute-start.53) | collective-permute-done | bytes 262176 | tf_op jit(solution)/shard_map/ppermute | solution.py:35
  247.0 2.8 %shard_map.109 = f32[16,4,8,128]{3,2,1,0:T(8,128)} custom-call(f32[2,128]{1,0:T(2,128)S(1)} %concatenate.6.flags, f32[16,4,8,128]{3,2,1,0:T(8,128)S(1)} %shard_map.108.state, f32[16,4,8,128]{3,2,1,0:T(8,128)S(1)} %collective-permute-done.52.on, f32[16,4,8,128]{3,2,1,0:T(8,128)S(1)} %collective-permute-done.53.off, f32[16,2,8,128]{3,2,1,0:T(8,128)S(1)} %slice.31.speed, ...), custom_call_target="tpu_custom_call" | custom-call | tf_op jit(solution)/shard_map/pallas_call | solution.py:39
  249.8 3.7 %all-to-all-start.1 = ((f32[16,4,8,128]{3,2,1,0:T(8,128)}), f32[16,4,8,128]{3,2,1,0:T(8,128)S(1)}, u32[]{:S(2)}, u32[]{:S(2)}) async-start(f32[16,4,8,128]{3,2,1,0:T(8,128)} %shard_map.109), calls=%async_computation.1 | async-start | bytes 524288 | tf_op jit(solution)/shard_map/all_to_all | solution.py:419
  254.9 6.0 %all-to-all-done.1.coarse = f32[16,4,8,128]{3,2,1,0:T(8,128)S(1)} async-done(((f32[16,4,8,128]{3,2,1,0:T(8,128)}), f32[16,4,8,128]{3,2,1,0:T(8,128)S(1)}, u32[]{:S(2)}, u32[]{:S(2)}) %all-to-all-start.1) | async-done | bytes 262176 | tf_op jit(solution)/shard_map/all_to_all | solution.py:419
  (166 shorter events, 133.4 us)
Async XLA Ops:
  2.6 11.5 %collective-permute-start.2 = (f32[256,256]{1,0:T(8,128)S(1)}, f32[256,256]{1,0:T(8,128)S(1)}, u32[]{:S(2)}, u32[]{:S(2)}) collective-permute-start(f32[256,256]{1,0:T(8,128)S(1)} %get-tuple-element.144), channel_id=1, source_target_pairs={{0,1},{1,0},{2,3},{3,2},{4,5},{5,4},{6,7},{7,6},{8,9},{9,8},{10,11... | collective-permute-start | bytes 786440 | tf_op jit(solution)/shard_map/ppermute | solution.py:35
  3.3 8.4 %collective-permute-start.1 = (f32[256,256]{1,0:T(8,128)}, f32[256,256]{1,0:T(8,128)S(1)}, u32[]{:S(2)}, u32[]{:S(2)}) collective-permute-start(f32[256,256]{1,0:T(8,128)} %get-tuple-element.145), channel_id=1, source_target_pairs={{1,2},{2,1},{3,4},{4,3},{5,6},{6,5},{7,8},{8,7},{9,10},{10,9},{11,... | collective-permute-start | bytes 786440 | tf_op jit(solution)/shard_map/ppermute | solution.py:35
  12.1 8.1 %collective-permute-start.3 = (f32[256,256]{1,0:T(8,128)S(1)}, f32[256,256]{1,0:T(8,128)S(1)}, u32[]{:S(2)}, u32[]{:S(2)}) collective-permute-start(f32[256,256]{1,0:T(8,128)S(1)} %shard_map.69.e0.b0), channel_id=1, source_target_pairs={{1,2},{2,1},{3,4},{4,3},{5,6},{6,5},{7,8},{8,7},{9,10},{10,9},{11,... | collective-permute-start | bytes 786440 | tf_op jit(solution)/shard_map/ppermute | solution.py:35
  15.6 7.4 %collective-permute-start.4 = (f32[256,256]{1,0:T(8,128)S(1)}, f32[256,256]{1,0:T(8,128)S(1)}, u32[]{:S(2)}, u32[]{:S(2)}) collective-permute-start(f32[256,256]{1,0:T(8,128)S(1)} %get-tuple-element.84), channel_id=1, source_target_pairs={{0,1},{1,0},{2,3},{3,2},{4,5},{5,4},{6,7},{7,6},{8,9},{9,8},{10,11... | collective-permute-start | bytes 786440 | tf_op jit(solution)/shard_map/ppermute | solution.py:35
  20.5 7.0 %collective-permute-start.5 = (f32[256,256]{1,0:T(8,128)S(1)}, f32[256,256]{1,0:T(8,128)S(1)}, u32[]{:S(2)}, u32[]{:S(2)}) collective-permute-start(f32[256,256]{1,0:T(8,128)S(1)} %shard_map.71.e0.b0), channel_id=1, source_target_pairs={{1,2},{2,1},{3,4},{4,3},{5,6},{6,5},{7,8},{8,7},{9,10},{10,9},{11,... | collective-permute-start | bytes 786440 | tf_op jit(solution)/shard_map/ppermute | solution.py:35
  27.8 6.9 %collective-permute-start.7 = (f32[256,256]{1,0:T(8,128)S(1)}, f32[256,256]{1,0:T(8,128)S(1)}, u32[]{:S(2)}, u32[]{:S(2)}) collective-permute-start(f32[256,256]{1,0:T(8,128)S(1)} %shard_map.73.e0.b0), channel_id=1, source_target_pairs={{1,2},{2,1},{3,4},{4,3},{5,6},{6,5},{7,8},{8,7},{9,10},{10,9},{11,... | collective-permute-start | bytes 786440 | tf_op jit(solution)/shard_map/ppermute | solution.py:35
  34.9 6.9 %collective-permute-start.9 = (f32[256,256]{1,0:T(8,128)S(1)}, f32[256,256]{1,0:T(8,128)S(1)}, u32[]{:S(2)}, u32[]{:S(2)}) collective-permute-start(f32[256,256]{1,0:T(8,128)S(1)} %shard_map.75.e0.b0), channel_id=1, source_target_pairs={{1,2},{2,1},{3,4},{4,3},{5,6},{6,5},{7,8},{8,7},{9,10},{10,9},{11,... | collective-permute-start | bytes 786440 | tf_op jit(solution)/shard_map/ppermute | solution.py:35
  42.1 6.9 %collective-permute-start.11 = (f32[256,256]{1,0:T(8,128)S(1)}, f32[256,256]{1,0:T(8,128)S(1)}, u32[]{:S(2)}, u32[]{:S(2)}) collective-permute-start(f32[256,256]{1,0:T(8,128)S(1)} %shard_map.78.e0.b0), channel_id=1, source_target_pairs={{1,2},{2,1},{3,4},{4,3},{5,6},{6,5},{7,8},{8,7},{9,10},{10,9},{11,... | collective-permute-start | bytes 786440 | tf_op jit(solution)/shard_map/ppermute | solution.py:35
  49.3 6.9 %collective-permute-start.13 = (f32[256,256]{1,0:T(8,128)S(1)}, f32[256,256]{1,0:T(8,128)S(1)}, u32[]{:S(2)}, u32[]{:S(2)}) collective-permute-start(f32[256,256]{1,0:T(8,128)S(1)} %shard_map.80.e0.b0), channel_id=1, source_target_pairs={{1,2},{2,1},{3,4},{4,3},{5,6},{6,5},{7,8},{8,7},{9,10},{10,9},{11,... | collective-permute-start | bytes 786440 | tf_op jit(solution)/shard_map/ppermute | solution.py:35
  56.4 6.9 %collective-permute-start.15 = (f32[256,256]{1,0:T(8,128)S(1)}, f32[256,256]{1,0:T(8,128)S(1)}, u32[]{:S(2)}, u32[]{:S(2)}) collective-permute-start(f32[256,256]{1,0:T(8,128)S(1)} %shard_map.82.e0.b0), channel_id=1, source_target_pairs={{1,2},{2,1},{3,4},{4,3},{5,6},{6,5},{7,8},{8,7},{9,10},{10,9},{11,... | collective-permute-start | bytes 786440 | tf_op jit(solution)/shard_map/ppermute | solution.py:35
  63.6 7.8 %collective-permute-start.17 = (f32[256,256]{1,0:T(8,128)S(1)}, f32[256,256]{1,0:T(8,128)S(1)}, u32[]{:S(2)}, u32[]{:S(2)}) collective-permute-start(f32[256,256]{1,0:T(8,128)S(1)} %shard_map.84.e0.b0), channel_id=1, source_target_pairs={{1,2},{2,1},{3,4},{4,3},{5,6},{6,5},{7,8},{8,7},{9,10},{10,9},{11,... | collective-permute-start | bytes 786440 | tf_op jit(solution)/shard_map/ppermute | solution.py:35
  67.8 10.0 %collective-permute-start.20 = (f32[2,2,128,128]{3,2,1,0:T(8,128)S(1)}, f32[2,2,128,128]{3,2,1,0:T(8,128)S(1)}, u32[]{:S(2)}, u32[]{:S(2)}) collective-permute-start(f32[2,2,128,128]{3,2,1,0:T(8,128)S(1)} %get-tuple-element.114), channel_id=1, source_target_pairs={{0,16},{16,32},{32,48},{48,64},{64,80},{80,96},{96,112},{112,0},{1... | collective-permute-start | bytes 786440 | tf_op jit(solution)/shard_map/ppermute | solution.py:360
  71.6 7.8 %collective-permute-start.19 = (f32[256,256]{1,0:T(8,128)S(1)}, f32[256,256]{1,0:T(8,128)S(1)}, u32[]{:S(2)}, u32[]{:S(2)}) collective-permute-start(f32[256,256]{1,0:T(8,128)S(1)} %shard_map.86.e0.b0), channel_id=1, source_target_pairs={{1,2},{2,1},{3,4},{4,3},{5,6},{6,5},{7,8},{8,7},{9,10},{10,9},{11,... | collective-permute-start | bytes 786440 | tf_op jit(solution)/shard_map/ppermute | solution.py:35
  79.7 7.0 %collective-permute-start.22 = (f32[256,256]{1,0:T(8,128)S(1)}, f32[256,256]{1,0:T(8,128)S(1)}, u32[]{:S(2)}, u32[]{:S(2)}) collective-permute-start(f32[256,256]{1,0:T(8,128)S(1)} %shard_map.88.e0.b0), channel_id=1, source_target_pairs={{1,2},{2,1},{3,4},{4,3},{5,6},{6,5},{7,8},{8,7},{9,10},{10,9},{11,... | collective-permute-start | bytes 786440 | tf_op jit(solution)/shard_map/ppermute | solution.py:35
  87.0 6.9 %collective-permute-start.24 = (f32[256,256]{1,0:T(8,128)S(1)}, f32[256,256]{1,0:T(8,128)S(1)}, u32[]{:S(2)}, u32[]{:S(2)}) collective-permute-start(f32[256,256]{1,0:T(8,128)S(1)} %shard_map.90.e0.b0), channel_id=1, source_target_pairs={{1,2},{2,1},{3,4},{4,3},{5,6},{6,5},{7,8},{8,7},{9,10},{10,9},{11,... | collective-permute-start | bytes 786440 | tf_op jit(solution)/shard_map/ppermute | solution.py:35
  94.2 6.9 %collective-permute-start.26 = (f32[256,256]{1,0:T(8,128)S(1)}, f32[256,256]{1,0:T(8,128)S(1)}, u32[]{:S(2)}, u32[]{:S(2)}) collective-permute-start(f32[256,256]{1,0:T(8,128)S(1)} %shard_map.92.e0.b0), channel_id=1, source_target_pairs={{1,2},{2,1},{3,4},{4,3},{5,6},{6,5},{7,8},{8,7},{9,10},{10,9},{11,... | collective-permute-start | bytes 786440 | tf_op jit(solution)/shard_map/ppermute | solution.py:35
  108.5 6.9 %collective-permute-start.30 = (f32[256,256]{1,0:T(8,128)S(1)}, f32[256,256]{1,0:T(8,128)S(1)}, u32[]{:S(2)}, u32[]{:S(2)}) collective-permute-start(f32[256,256]{1,0:T(8,128)S(1)} %shard_map.96.e0.b0), channel_id=1, source_target_pairs={{1,2},{2,1},{3,4},{4,3},{5,6},{6,5},{7,8},{8,7},{9,10},{10,9},{11,... | collective-permute-start | bytes 786440 | tf_op jit(solution)/shard_map/ppermute | solution.py:35
  115.7 6.9 %collective-permute-start.32 = (f32[256,256]{1,0:T(8,128)S(1)}, f32[256,256]{1,0:T(8,128)S(1)}, u32[]{:S(2)}, u32[]{:S(2)}) collective-permute-start(f32[256,256]{1,0:T(8,128)S(1)} %shard_map.98.e0.b0), channel_id=1, source_target_pairs={{1,2},{2,1},{3,4},{4,3},{5,6},{6,5},{7,8},{8,7},{9,10},{10,9},{11,... | collective-permute-start | bytes 786440 | tf_op jit(solution)/shard_map/ppermute | solution.py:35
  143.2 13.6 %collective-permute-start.34 = (f32[16,5,8,128]{3,2,1,0:T(8,128)S(1)}, f32[16,5,8,128]{3,2,1,0:T(8,128)S(1)}, u32[]{:S(2)}, u32[]{:S(2)}) collective-permute-start(f32[16,5,8,128]{3,2,1,0:T(8,128)S(1)} %slice.30.rest_0_), channel_id=1, source_target_pairs={{0,112},{16,0},{32,16},{48,32},{64,48},{80,64},{96,80},{112,96},{1... | collective-permute-start | bytes 983048 | tf_op jit(solution)/shard_map/ppermute | solution.py:406
  169.5 11.4 %collective-permute-start.39 = (f32[16,4,8,128]{3,2,1,0:T(8,128)S(1)}, f32[16,4,8,128]{3,2,1,0:T(8,128)S(1)}, u32[]{:S(2)}, u32[]{:S(2)}) collective-permute-start(f32[16,4,8,128]{3,2,1,0:T(8,128)S(1)} %shard_map.103.rest_0_), channel_id=1, source_target_pairs={{32,0},{48,16},{64,32},{80,48},{96,64},{112,80},{0,96},{16,112},{3... | collective-permute-start | bytes 786440 | tf_op jit(solution)/shard_map/ppermute | solution.py:402
  199.3 8.8 %collective-permute-start.44 = (f32[16,4,8,128]{3,2,1,0:T(8,128)S(1)}, f32[16,4,8,128]{3,2,1,0:T(8,128)S(1)}, u32[]{:S(2)}, u32[]{:S(2)}) collective-permute-start(f32[16,4,8,128]{3,2,1,0:T(8,128)S(1)} %shard_map.105), channel_id=1, source_target_pairs={{80,0},{96,16},{112,32},{0,48},{16,64},{32,80},{48,96},{64,112},{8... | collective-permute-start | bytes 786440 | tf_op jit(solution)/shard_map/ppermute | solution.py:402
  218.0 11.7 %collective-permute-start.48 = (f32[16,4,8,128]{3,2,1,0:T(8,128)S(1)}, f32[16,4,8,128]{3,2,1,0:T(8,128)S(1)}, u32[]{:S(2)}, u32[]{:S(2)}) collective-permute-start(f32[16,4,8,128]{3,2,1,0:T(8,128)S(1)} %shard_map.106.state), channel_id=1, source_target_pairs={{1,2},{2,1},{3,6},{6,3},{7,4},{4,7},{5,8},{8,5},{9,10},{10,9},{11,... | collective-permute-start | bytes 786440 | tf_op jit(solution)/shard_map/ppermute | solution.py:35
  218.0 13.8 %collective-permute-start.49 = (f32[16,4,8,128]{3,2,1,0:T(8,128)S(1)}, f32[16,4,8,128]{3,2,1,0:T(8,128)S(1)}, u32[]{:S(2)}, u32[]{:S(2)}) collective-permute-start(f32[16,4,8,128]{3,2,1,0:T(8,128)S(1)} %shard_map.105), channel_id=1, source_target_pairs={{0,112},{16,0},{32,16},{48,32},{64,48},{80,64},{96,80},{112,96},{1... | collective-permute-start | bytes 786440 | tf_op jit(solution)/shard_map/ppermute | solution.py:414
  249.8 11.1 %all-to-all-start.1 = ((f32[16,4,8,128]{3,2,1,0:T(8,128)}), f32[16,4,8,128]{3,2,1,0:T(8,128)S(1)}, u32[]{:S(2)}, u32[]{:S(2)}) async-start(f32[16,4,8,128]{3,2,1,0:T(8,128)} %shard_map.109), calls=%async_computation.1 | async-start | bytes 524288 | tf_op jit(solution)/shard_map/all_to_all | solution.py:419
  (41 other events, 175.1 us)
where the time goes:
time: 263 us
  waiting for transfers between devices  124 us (47%)
  starting transfers between devices  61.6 us (23%)
  Pallas kernels  50.9 us (19%)
  blocking collectives  16.9 us (6%)
  local copies, waits for them, and re-layouts  6.31 us (2%)
    ppermute x48, waiting for transfers between devices, exchange(): return lax.ppermute(block, ('tm', 'space'), pairs)  87 us
    pallas_call x43, Pallas kernels, call(): pl.pallas_call(kernel, out_shape=out_shapes, in_specs=specs, out_specs=ja...  50.9 us
    ppermute x48, starting transfers between devices, exchange(): return lax.ppermute(block, ('tm', 'space'), pairs)  49.9 us
    ppermute x2, waiting for transfers between devices, later(): lax.ppermute(state, 'tm', route)  20 us
    all_to_all x1, blocking collectives, body(): pieces = lax.all_to_all(pieces, 'space', 0, 0)  16.9 us
    ppermute x1, waiting for transfers between devices, body(): moved = lax.ppermute(pieces, 'tm', back)  7.69 us
    all_to_all x1, waiting for transfers between devices, body(): coarse = lax.all_to_all(moved, 'space', 0, 0)  6.05 us
  transfers between devices with their start and end apart: 55, of which 35 were waited for; matrix products, arithmetic and copies ran while one was open for 1% of the time, Pallas kernels for 12%

commit v1 on v0

--- a/solution.py
+++ b/solution.py
@@ -14,25 +14,40 @@
 UNROLL = 8
 HIGH = lax.Precision.HIGHEST
 
-SNAKE = tuple(
-    y * 4 + z * 2 + c for y in range(4) for z in ((0, 1) if y % 2 == 0 else (1, 0)) for c in (0, 1)
+TOUR = tuple(y * 4 + c for y in range(4) for c in (0, 1)) + tuple(
+    y * 4 + 2 + c for y in reversed(range(4)) for c in (0, 1)
 )
-PLACE = tuple(SNAKE.index(s) for s in range(SLABS))
+TOUR = TOUR[1:] + TOUR[:1]
+PLACE = tuple(TOUR.index(s) for s in range(SLABS))
 VM = pl.BlockSpec(memory_space=pltpu.VMEM)
 SM = pl.BlockSpec(memory_space=pltpu.SMEM)
 HB = pl.BlockSpec(memory_space=pltpu.HBM)
 
 
-def exchange(block, order, offset):
-    pairs = []
+def trade(block, pairs, ends=()):
+    route = []
     for row in range(GROUPS):
         base, beside = row * SLABS, (row ^ 1) * SLABS
-        for i in range(offset, SLABS - 1, 2):
-            here, there = base + order[i], base + order[i + 1]
-            pairs += [(here, there), (there, here)]
-        if offset:
-            pairs += [(base + end, beside + end) for end in (order[0], order[-1])]
-    return lax.ppermute(block, ("tm", "space"), pairs)
+        for here, there in pairs:
+            route += [(base + here, base + there), (base + there, base + here)]
+        route += [(base + end, beside + end) for end in ends]
+    return lax.ppermute(block, ("tm", "space"), route)
+
+
+def away_side(block):
+    return trade(block, [(TOUR[i], TOUR[i + 1]) for i in range(0, SLABS, 2)])
+
+
+def chip_side(block):
+    return trade(block, [(TOUR[i], TOUR[(i + 1) % SLABS]) for i in range(1, SLABS, 2)])
+
+
+def off_chip(plane):
+    return trade(plane, [(i, i + 1) for i in range(1, SLABS - 1, 2)], (0, SLABS - 1))
+
+
+def on_chip(plane):
+    return trade(plane, [(i, i + 1) for i in range(0, SLABS, 2)])
 
 
 def call(kernel, out_shapes, args, specs, scratch=(), aliases=None, cost=None):
@@ -115,6 +130,31 @@
     return row
 
 
+def first_kernel(info, states, off, on, sems):
+    def fetch(near, far):
+        copies = [
+            pltpu.make_async_copy(states.at[0, near], off, sems.at[0]),
+            pltpu.make_async_copy(states.at[0, far], on, sems.at[1]),
+        ]
+        for copy in copies:
+            copy.start()
+        for copy in copies:
+            copy.wait()
+
+    @pl.when(info[0] == 1)
+    def _():
+        fetch(3, 0)
+
+    @pl.when(info[0] == 0)
+    def _():
+        fetch(0, 3)
+
+    @pl.when(info[2] == 0)
+    def _():
+        off[...] = jnp.zeros_like(off)
+        on[...] = jnp.zeros_like(on)
+
+
 def prep_kernel(info, courant, misfit, states, ce, ci, fe, fi, e0, inner, b0, binner, sems):
     def spread(flip):
         q = (lambda k: 3 - k) if flip else (lambda k: k)
@@ -226,8 +266,8 @@
     a[0], a[nx + 1], b[0], b[nx + 1] = zero, zero, zero, zero
 
     def fill(target, mine, other, far):
-        far = far.reshape(nx, block, nz) * near
-        other = other.reshape(nx, block, nz)
+        far = far.reshape(nx, block, nz)
+        other = other.reshape(nx, block, nz) * near
         target(slice(0, block), jnp.where(odd, other, far))
         target(slice(block, 2 * block), mine.reshape(nx, block, nz))
         target(slice(2 * block, tall), jnp.where(odd, far, other))
@@ -301,30 +341,34 @@
     slab = lax.axis_index("space")
     tm = lax.axis_index("tm")
     states = boundary_states[0]
-    natural = tuple(range(SLABS))
     odd = lax.rem(slab, 2)
     alive = (tm > 0).astype(jnp.int32)
     reach = ((slab > 0) & (slab < SLABS - 1)).astype(jnp.int32)
-    creach = ((slab != SNAKE[0]) & (slab != SNAKE[-1])).astype(jnp.int32)
+    creach = ((slab != TOUR[0]) & (slab != TOUR[-1])).astype(jnp.int32)
     info = jnp.stack([odd, slab, alive, reach, creach]).astype(jnp.int32)
     ring = [(i, (i + 1) % GROUPS) for i in range(GROUPS)]
     back = [(i, (i - 1) % GROUPS) for i in range(GROUPS)]
 
-    mask = alive.astype(jnp.float32)
-    first_off = lax.dynamic_index_in_dim(states[0], 3 * odd, 0, keepdims=False) * mask
-    first_on = lax.dynamic_index_in_dim(states[0], 3 - 3 * odd, 0, keepdims=False) * mask
-    off = exchange(first_off, natural, 1)
-    on = exchange(first_on, natural, 0)
+    plane = f32(ny, nz)
+    in_hbm = [pltpu.with_memory_space_constraint(x, pltpu.HBM) for x in (courant, misfit, states)]
+    first_off, first_on = call(
+        first_kernel,
+        (plane, plane),
+        (info, in_hbm[2]),
+        [SM, HB],
+        scratch=[pltpu.SemaphoreType.DMA((2,))],
+    )
+    off = off_chip(first_off)
+    on = on_chip(first_on)
     wave, marks, _ = lax.optimization_barrier((wavelet, source_cells, first_off))
     packed = lax.ppermute(jnp.stack([wave, marks.astype(jnp.float32)]), "tm", ring)
     weights = jnp.broadcast_to(packed[0][:, None], (steps, nz))
     cells = packed[1].astype(jnp.int32)
 
-    plane = f32(ny, nz)
     ce, ci, fe, fi, e0, inner, b0, binner = call(
         prep_kernel,
         (plane, f32(3, ny, nz)) * 4,
-        (info, courant, misfit, states),
+        (info, *in_hbm),
         [SM, HB, HB, HB],
         scratch=[pltpu.SemaphoreType.DMA((16,))],
     )
@@ -339,7 +383,7 @@
             [VM] * 8,
         )
         if turn < steps - 1:
-            off = exchange(n0, natural, 1)
+            off = off_chip(n0)
         n1, ninner, samples = call(
             functools.partial(inner_kernel, level, level + 1 if turn else None),
             (plane, f32(3, ny, nz), f32(steps, nz)),
@@ -361,7 +405,7 @@
         if turn == 8:
             n1, rb = lax.optimization_barrier((n1, rb))
         if turn < steps - 1:
-            on = exchange(n1, natural, 0)
+            on = on_chip(n1)
         e0, inner, b0, binner = n0, ninner, e0, inner
 
     pieces = call(
@@ -380,7 +424,7 @@
     flags = jnp.concatenate([parity, near], axis=0)
 
     def phi(state, add=None):
-        sides = (exchange(state, SNAKE, 1), exchange(state, SNAKE, 0))
+        sides = (away_side(state), chip_side(state))
         nx = SLABS * 2
         args = (flags, state, sides[1], sides[0], speed, son, soff)
         args = args + (() if add is None else (add,))
@@ -401,11 +445,12 @@
         group = tm if aligned else lax.rem(tm + GROUPS - 1, GROUPS)
         return lax.ppermute(state, "tm", route) * (group + distance < GROUPS).astype(jnp.float32)
 
-    soff = exchange(speed, SNAKE, 1)
-    son = exchange(speed, SNAKE, 0)
+    soff = away_side(speed)
+    son = chip_side(speed)
     moved = lax.ppermute(pieces, "tm", back)
     moved, son, soff = lax.optimization_barrier((moved, son, soff))
-    gradient = jnp.sum(moved[:, 4, 0, :steps], axis=0)
+    gradient = jnp.sum(moved[:, 4, 0, :], axis=0)[:steps]
+    moved, gradient = lax.optimization_barrier((moved, gradient))
     moved = moved[:, :4] * (lax.rem(tm + GROUPS - 1, GROUPS) + 1 < GROUPS).astype(jnp.float32)
     total = phi(moved, pieces)
     moved = later(total, 2, False)

time: 263 us -> 259 us (0.985)
  blocking collectives: 16.9 us -> 27.2 us
  waiting for transfers between devices: 124 us -> 116 us
  local copies, waits for them, and re-layouts: 6.31 us -> 1.93 us
  starting transfers between devices: 61.6 us -> 58.6 us
    all_to_all x0 -> x1, blocking collectives: none -> 10.2 us  [body(): coarse = lax.all_to_all(moved, 'space', 0, 0)]
    ppermute x48, waiting for transfers between devices: 87 us -> 80.4 us  [trade(): return lax.ppermute(block, ('tm', 'space'), route)]
    all_to_all x1 -> x0, waiting for transfers between devices: 6.05 us -> none  [body(): coarse = lax.all_to_all(moved, 'space', 0, 0)]
    all_to_all x1 -> x0, starting transfers between devices: 3.71 us -> none  [body(): coarse = lax.all_to_all(moved, 'space', 0, 0)]
    unnamed x18 -> x12, local copies, waits for them, and re-layouts: 4.84 us -> 1.67 us
    ppermute x1, waiting for transfers between devices: 0.01 us -> 3.17 us  [body(): own = lax.ppermute(total, 'tm', back)]
    pallas_call x43 -> x44, Pallas kernels: 50.9 us -> 53.4 us  [call(): pl.pallas_call(kernel, out_shape=out_shapes, in_specs=specs, out_specs=ja...]
  transfers between devices with their start and end apart: 55 -> 54, of which waited for: 35 -> 34; matrix products, arithmetic and copies ran while one was open for 1% -> 0% of each run, Pallas kernels for 12% -> 13%
where the time goes in v1:
time: 259 us; the launch traced here: 258 us
  waiting for transfers between devices  116 us (45%)
  starting transfers between devices  58.6 us (23%)
  Pallas kernels  53.4 us (21%)
  blocking collectives  27.2 us (11%)
    ppermute x48, waiting for transfers between devices, trade(): return lax.ppermute(block, ('tm', 'space'), route)  80.4 us
    pallas_call x44, Pallas kernels, call(): pl.pallas_call(kernel, out_shape=out_shapes, in_specs=specs, out_specs=ja...  53.4 us
    ppermute x48, starting transfers between devices, trade(): return lax.ppermute(block, ('tm', 'space'), route)  51.2 us
    ppermute x2, waiting for transfers between devices, later(): lax.ppermute(state, 'tm', route)  20.5 us
    all_to_all x1, blocking collectives, body(): pieces = lax.all_to_all(pieces, 'space', 0, 0)  16.9 us
    all_to_all x1, blocking collectives, body(): coarse = lax.all_to_all(moved, 'space', 0, 0)  10.2 us
    ppermute x1, waiting for transfers between devices, body(): moved = lax.ppermute(pieces, 'tm', back)  8.17 us
  transfers between devices with their start and end apart: 54, of which 34 were waited for; matrix products, arithmetic and copies ran while one was open for 0% of the time, Pallas kernels for 13%

profile of v1, /device:TPU:7, one launch (start us, length us, event | category | flops | bytes accessed | tf_op | source)
XLA Modules:
  0.0 258.5 jit_solution(3062405572470372479)
XLA Ops:
  4.8 3.3 %collective-permute-start = (f32[2,16]{1,0:T(2,128)S(1)}, f32[2,16]{1,0:T(2,128)S(1)}, u32[]{:S(2)}, u32[]{:S(2)}) collective-permute-start(f32[2,16]{1,0:T(2,128)S(1)} %pad_maximum_fusion), channel_id=1, source_target_pairs={{0,16},{16,32},{32,48},{48,64},{64,80},{80,96},{96,112},{112,0},{1... | collective-permute-start | bytes 392 | tf_op jit(solution)/shard_map/ppermute | solution.py:364
  8.0 2.8 %shard_map.69 = (f32[256,256]{1,0:T(8,128)S(1)}, f32[3,256,256]{2,1,0:T(8,128)S(1)}, f32[256,256]{1,0:T(8,128)S(1)}, f32[3,256,256]{2,1,0:T(8,128)S(1)}, f32[256...) custom-call(s32[5]{0:T(128)S(1)} %stack.36.info, ...), custom_call_target="tpu_custom_call" | custom-call | tf_op jit(solution)/shard_map/pallas_call | solution.py:54
  15.4 4.2 %collective-permute-done.3.off = f32[256,256]{1,0:T(8,128)S(1)} collective-permute-done((f32[256,256]{1,0:T(8,128)S(1)}, f32[256,256]{1,0:T(8,128)S(1)}, u32[]{:S(2)}, u32[]{:S(2)}) %collective-permute-start.3) | collective-permute-done | bytes 262176 | tf_op jit(solution)/shard_map/ppermute | solution.py:34
  52.7 2.7 %collective-permute-done.13.off = f32[256,256]{1,0:T(8,128)S(1)} collective-permute-done((f32[256,256]{1,0:T(8,128)S(1)}, f32[256,256]{1,0:T(8,128)S(1)}, u32[]{:S(2)}, u32[]{:S(2)}) %collective-permute-start.13) | collective-permute-done | bytes 262176 | tf_op jit(solution)/shard_map/ppermute | solution.py:34
  59.9 2.7 %collective-permute-done.15.off = f32[256,256]{1,0:T(8,128)S(1)} collective-permute-done((f32[256,256]{1,0:T(8,128)S(1)}, f32[256,256]{1,0:T(8,128)S(1)}, u32[]{:S(2)}, u32[]{:S(2)}) %collective-permute-start.15) | collective-permute-done | bytes 262176 | tf_op jit(solution)/shard_map/ppermute | solution.py:34
  67.0 3.9 %collective-permute-start.20 = (f32[2,2,128,128]{3,2,1,0:T(8,128)S(1)}, f32[2,2,128,128]{3,2,1,0:T(8,128)S(1)}, u32[]{:S(2)}, u32[]{:S(2)}) collective-permute-start(f32[2,2,128,128]{3,2,1,0:T(8,128)S(1)} %get-tuple-element.120), channel_id=1, source_target_pairs={{0,16},{16,32},{32,48},{48,64},{64,80},{80,96},{96,112},{112,0},{1... | collective-permute-start | bytes 786440 | tf_op jit(solution)/shard_map/ppermute | solution.py:404
  74.3 3.3 %collective-permute-done.20.rb = f32[2,2,128,128]{3,2,1,0:T(8,128)S(1)} collective-permute-done((f32[2,2,128,128]{3,2,1,0:T(8,128)S(1)}, f32[2,2,128,128]{3,2,1,0:T(8,128)S(1)}, u32[]{:S(2)}, u32[]{:S(2)}) %collective-permute-start.20) | collective-permute-done | bytes 262176 | tf_op jit(solution)/shard_map/ppermute | solution.py:404
  83.4 3.3 %collective-permute-done.22.off = f32[256,256]{1,0:T(8,128)S(1)} collective-permute-done((f32[256,256]{1,0:T(8,128)S(1)}, f32[256,256]{1,0:T(8,128)S(1)}, u32[]{:S(2)}, u32[]{:S(2)}) %collective-permute-start.22) | collective-permute-done | bytes 262176 | tf_op jit(solution)/shard_map/ppermute | solution.py:34
  91.2 2.7 %collective-permute-done.24.off = f32[256,256]{1,0:T(8,128)S(1)} collective-permute-done((f32[256,256]{1,0:T(8,128)S(1)}, f32[256,256]{1,0:T(8,128)S(1)}, u32[]{:S(2)}, u32[]{:S(2)}) %collective-permute-start.24) | collective-permute-done | bytes 262176 | tf_op jit(solution)/shard_map/ppermute | solution.py:34
  126.2 16.9 %all_to_all.10 = f32[16,7,8,128]{3,2,1,0:T(8,128)S(1)} all-to-all(f32[16,7,8,128]{3,2,1,0:T(8,128)S(1)} %shard_map.103), channel_id=1, replica_groups=mesh['tm'=8,'space'=16] {'space'}, dimensions={0} | all-to-all | bytes 917504 | tf_op jit(solution)/shard_map/all_to_all | solution.py:418
  145.4 3.4 %collective-permute-done.36.soff = f32[16,2,8,128]{3,2,1,0:T(8,128)S(1)} collective-permute-done((f32[16,2,8,128]{3,2,1,0:T(8,128)S(1)}, f32[16,2,8,128]{3,2,1,0:T(8,128)S(1)}, u32[]{:S(2)}, u32[]{:S(2)}) %collective-permute-start.36) | collective-permute-done | bytes 131104 | tf_op jit(solution)/shard_map/ppermute | solution.py:34
  148.8 8.2 %collective-permute-done.34 = f32[16,5,8,128]{3,2,1,0:T(8,128)S(1)} collective-permute-done((f32[16,5,8,128]{3,2,1,0:T(8,128)S(1)}, f32[16,5,8,128]{3,2,1,0:T(8,128)S(1)}, u32[]{:S(2)}, u32[]{:S(2)}) %collective-permute-start.34) | collective-permute-done | bytes 327712 | tf_op jit(solution)/shard_map/ppermute | solution.py:450
  161.1 4.0 %collective-permute-done.38.off = f32[16,4,8,128]{3,2,1,0:T(8,128)} collective-permute-done((f32[16,4,8,128]{3,2,1,0:T(8,128)S(1)}, f32[16,4,8,128]{3,2,1,0:T(8,128)}, u32[]{:S(2)}, u32[]{:S(2)}) %collective-permute-start.38) | collective-permute-done | bytes 262176 | tf_op jit(solution)/shard_map/ppermute | solution.py:34
  166.2 3.0 %shard_map.104.rest_0_ = f32[16,4,8,128]{3,2,1,0:T(8,128)S(1)} custom-call(f32[2,128]{1,0:T(2,128)S(1)} %concatenate.6.flags, f32[16,4,8,128]{3,2,1,0:T(8,128)S(1)} %slice_multiply_fusion.state, f32[16,4,8,128]{3,2,1,0:T(8,128)S(1)} %copy-done.3, f32[16,4,8,128]{3,2,1,0:T(8,128)} %collective-permute-done.38.off, f32[16,2,8,128]{3,2,1,0:T(8,128)S(1)} %slice.29.speed, ...), custom_call_target="tpu_custom_call" | custom-call | tf_op jit(solution)/shard_map/pallas_call | solution.py:54
  169.3 11.7 %collective-permute-done.39 = f32[16,4,8,128]{3,2,1,0:T(8,128)S(1)} collective-permute-done((f32[16,4,8,128]{3,2,1,0:T(8,128)S(1)}, f32[16,4,8,128]{3,2,1,0:T(8,128)S(1)}, u32[]{:S(2)}, u32[]{:S(2)}) %collective-permute-start.39) | collective-permute-done | bytes 262176 | tf_op jit(solution)/shard_map/ppermute | solution.py:446
  183.2 4.6 %collective-permute-done.41.off = f32[16,4,8,128]{3,2,1,0:T(8,128)S(1)} collective-permute-done((f32[16,4,8,128]{3,2,1,0:T(8,128)S(1)}, f32[16,4,8,128]{3,2,1,0:T(8,128)S(1)}, u32[]{:S(2)}, u32[]{:S(2)}) %collective-permute-start.41) | collective-permute-done | bytes 262176 | tf_op jit(solution)/shard_map/ppermute | solution.py:34
  191.5 4.6 %collective-permute-done.43.off = f32[16,4,8,128]{3,2,1,0:T(8,128)S(1)} collective-permute-done((f32[16,4,8,128]{3,2,1,0:T(8,128)S(1)}, f32[16,4,8,128]{3,2,1,0:T(8,128)S(1)}, u32[]{:S(2)}, u32[]{:S(2)}) %collective-permute-start.43) | collective-permute-done | bytes 262176 | tf_op jit(solution)/shard_map/ppermute | solution.py:34
  198.3 8.9 %collective-permute-done.44 = f32[16,4,8,128]{3,2,1,0:T(8,128)S(1)} collective-permute-done((f32[16,4,8,128]{3,2,1,0:T(8,128)S(1)}, f32[16,4,8,128]{3,2,1,0:T(8,128)S(1)}, u32[]{:S(2)}, u32[]{:S(2)}) %collective-permute-start.44) | collective-permute-done | bytes 262176 | tf_op jit(solution)/shard_map/ppermute | solution.py:446
  209.5 4.6 %collective-permute-done.46.off = f32[16,4,8,128]{3,2,1,0:T(8,128)S(1)} collective-permute-done((f32[16,4,8,128]{3,2,1,0:T(8,128)S(1)}, f32[16,4,8,128]{3,2,1,0:T(8,128)S(1)}, u32[]{:S(2)}, u32[]{:S(2)}) %collective-permute-start.46) | collective-permute-done | bytes 262176 | tf_op jit(solution)/shard_map/ppermute | solution.py:34
  217.8 4.6 %collective-permute-done.48.off = f32[16,4,8,128]{3,2,1,0:T(8,128)S(1)} collective-permute-done((f32[16,4,8,128]{3,2,1,0:T(8,128)S(1)}, f32[16,4,8,128]{3,2,1,0:T(8,128)S(1)}, u32[]{:S(2)}, u32[]{:S(2)}) %collective-permute-start.48) | collective-permute-done | bytes 262176 | tf_op jit(solution)/shard_map/ppermute | solution.py:34
  224.5 3.2 %collective-permute-done.49.rest_0_ = f32[16,4,8,128]{3,2,1,0:T(8,128)S(1)} collective-permute-done((f32[16,4,8,128]{3,2,1,0:T(8,128)S(1)}, f32[16,4,8,128]{3,2,1,0:T(8,128)S(1)}, u32[]{:S(2)}, u32[]{:S(2)}) %collective-permute-start.49) | collective-permute-done | bytes 262176 | tf_op jit(solution)/shard_map/ppermute | solution.py:459
  231.5 4.6 %collective-permute-done.51.off = f32[16,4,8,128]{3,2,1,0:T(8,128)S(1)} collective-permute-done((f32[16,4,8,128]{3,2,1,0:T(8,128)S(1)}, f32[16,4,8,128]{3,2,1,0:T(8,128)S(1)}, u32[]{:S(2)}, u32[]{:S(2)}) %collective-permute-start.51) | collective-permute-done | bytes 262176 | tf_op jit(solution)/shard_map/ppermute | solution.py:34
  239.8 4.4 %collective-permute-done.53.off = f32[16,4,8,128]{3,2,1,0:T(8,128)S(1)} collective-permute-done((f32[16,4,8,128]{3,2,1,0:T(8,128)S(1)}, f32[16,4,8,128]{3,2,1,0:T(8,128)S(1)}, u32[]{:S(2)}, u32[]{:S(2)}) %collective-permute-start.53) | collective-permute-done | bytes 262176 | tf_op jit(solution)/shard_map/ppermute | solution.py:34
  246.3 10.2 %all_to_all.11.coarse = f32[16,4,8,128]{3,2,1,0:T(8,128)S(1)} all-to-all(f32[16,4,8,128]{3,2,1,0:T(8,128)S(1)} %shard_map.110), channel_id=1, replica_groups=mesh['tm'=8,'space'=16] {'space'}, dimensions={0} | all-to-all | bytes 524288 | tf_op jit(solution)/shard_map/all_to_all | solution.py:464
  (157 shorter events, 131.3 us)
Async XLA Ops:
  2.4 11.4 %collective-permute-start.2 = (f32[256,256]{1,0:T(8,128)S(1)}, f32[256,256]{1,0:T(8,128)S(1)}, u32[]{:S(2)}, u32[]{:S(2)}) collective-permute-start(f32[256,256]{1,0:T(8,128)S(1)} %get-tuple-element.86), channel_id=1, source_target_pairs={{0,1},{1,0},{2,3},{3,2},{4,5},{5,4},{6,7},{7,6},{8,9},{9,8},{10,11... | collective-permute-start | bytes 786440 | tf_op jit(solution)/shard_map/ppermute | solution.py:34
  3.1 7.8 %collective-permute-start.1 = (f32[256,256]{1,0:T(8,128)S(1)}, f32[256,256]{1,0:T(8,128)S(1)}, u32[]{:S(2)}, u32[]{:S(2)}) collective-permute-start(f32[256,256]{1,0:T(8,128)S(1)} %get-tuple-element.77), channel_id=1, source_target_pairs={{1,2},{2,1},{3,4},{4,3},{5,6},{6,5},{7,8},{8,7},{9,10},{10,9},{11,... | collective-permute-start | bytes 786440 | tf_op jit(solution)/shard_map/ppermute | solution.py:34
  11.3 8.3 %collective-permute-start.3 = (f32[256,256]{1,0:T(8,128)S(1)}, f32[256,256]{1,0:T(8,128)S(1)}, u32[]{:S(2)}, u32[]{:S(2)}) collective-permute-start(f32[256,256]{1,0:T(8,128)S(1)} %shard_map.70.e0.b0), channel_id=1, source_target_pairs={{1,2},{2,1},{3,4},{4,3},{5,6},{6,5},{7,8},{8,7},{9,10},{10,9},{11,... | collective-permute-start | bytes 786440 | tf_op jit(solution)/shard_map/ppermute | solution.py:34
  15.3 7.1 %collective-permute-start.4 = (f32[256,256]{1,0:T(8,128)S(1)}, f32[256,256]{1,0:T(8,128)S(1)}, u32[]{:S(2)}, u32[]{:S(2)}) collective-permute-start(f32[256,256]{1,0:T(8,128)S(1)} %get-tuple-element.90), channel_id=1, source_target_pairs={{0,1},{1,0},{2,3},{3,2},{4,5},{5,4},{6,7},{7,6},{8,9},{9,8},{10,11... | collective-permute-start | bytes 786440 | tf_op jit(solution)/shard_map/ppermute | solution.py:34
  19.9 6.9 %collective-permute-start.5 = (f32[256,256]{1,0:T(8,128)S(1)}, f32[256,256]{1,0:T(8,128)S(1)}, u32[]{:S(2)}, u32[]{:S(2)}) collective-permute-start(f32[256,256]{1,0:T(8,128)S(1)} %shard_map.72.e0.b0), channel_id=1, source_target_pairs={{1,2},{2,1},{3,4},{4,3},{5,6},{6,5},{7,8},{8,7},{9,10},{10,9},{11,... | collective-permute-start | bytes 786440 | tf_op jit(solution)/shard_map/ppermute | solution.py:34
  24.0 6.6 %collective-permute-start.6 = (f32[256,256]{1,0:T(8,128)S(1)}, f32[256,256]{1,0:T(8,128)S(1)}, u32[]{:S(2)}, u32[]{:S(2)}) collective-permute-start(f32[256,256]{1,0:T(8,128)S(1)} %get-tuple-element.93), channel_id=1, source_target_pairs={{0,1},{1,0},{2,3},{3,2},{4,5},{5,4},{6,7},{7,6},{8,9},{9,8},{10,11... | collective-permute-start | bytes 786440 | tf_op jit(solution)/shard_map/ppermute | solution.py:34
  27.0 6.9 %collective-permute-start.7 = (f32[256,256]{1,0:T(8,128)S(1)}, f32[256,256]{1,0:T(8,128)S(1)}, u32[]{:S(2)}, u32[]{:S(2)}) collective-permute-start(f32[256,256]{1,0:T(8,128)S(1)} %shard_map.74.e0.b0), channel_id=1, source_target_pairs={{1,2},{2,1},{3,4},{4,3},{5,6},{6,5},{7,8},{8,7},{9,10},{10,9},{11,... | collective-permute-start | bytes 786440 | tf_op jit(solution)/shard_map/ppermute | solution.py:34
  34.2 6.9 %collective-permute-start.9 = (f32[256,256]{1,0:T(8,128)S(1)}, f32[256,256]{1,0:T(8,128)S(1)}, u32[]{:S(2)}, u32[]{:S(2)}) collective-permute-start(f32[256,256]{1,0:T(8,128)S(1)} %shard_map.76.e0.b0), channel_id=1, source_target_pairs={{1,2},{2,1},{3,4},{4,3},{5,6},{6,5},{7,8},{8,7},{9,10},{10,9},{11,... | collective-permute-start | bytes 786440 | tf_op jit(solution)/shard_map/ppermute | solution.py:34
  41.4 6.9 %collective-permute-start.11 = (f32[256,256]{1,0:T(8,128)S(1)}, f32[256,256]{1,0:T(8,128)S(1)}, u32[]{:S(2)}, u32[]{:S(2)}) collective-permute-start(f32[256,256]{1,0:T(8,128)S(1)} %shard_map.79.e0.b0), channel_id=1, source_target_pairs={{1,2},{2,1},{3,4},{4,3},{5,6},{6,5},{7,8},{8,7},{9,10},{10,9},{11,... | collective-permute-start | bytes 786440 | tf_op jit(solution)/shard_map/ppermute | solution.py:34
  48.5 6.9 %collective-permute-start.13 = (f32[256,256]{1,0:T(8,128)S(1)}, f32[256,256]{1,0:T(8,128)S(1)}, u32[]{:S(2)}, u32[]{:S(2)}) collective-permute-start(f32[256,256]{1,0:T(8,128)S(1)} %shard_map.81.e0.b0), channel_id=1, source_target_pairs={{1,2},{2,1},{3,4},{4,3},{5,6},{6,5},{7,8},{8,7},{9,10},{10,9},{11,... | collective-permute-start | bytes 786440 | tf_op jit(solution)/shard_map/ppermute | solution.py:34
  55.7 6.9 %collective-permute-start.15 = (f32[256,256]{1,0:T(8,128)S(1)}, f32[256,256]{1,0:T(8,128)S(1)}, u32[]{:S(2)}, u32[]{:S(2)}) collective-permute-start(f32[256,256]{1,0:T(8,128)S(1)} %shard_map.83.e0.b0), channel_id=1, source_target_pairs={{1,2},{2,1},{3,4},{4,3},{5,6},{6,5},{7,8},{8,7},{9,10},{10,9},{11,... | collective-permute-start | bytes 786440 | tf_op jit(solution)/shard_map/ppermute | solution.py:34
  62.9 8.1 %collective-permute-start.17 = (f32[256,256]{1,0:T(8,128)S(1)}, f32[256,256]{1,0:T(8,128)S(1)}, u32[]{:S(2)}, u32[]{:S(2)}) collective-permute-start(f32[256,256]{1,0:T(8,128)S(1)} %shard_map.85.e0.b0), channel_id=1, source_target_pairs={{1,2},{2,1},{3,4},{4,3},{5,6},{6,5},{7,8},{8,7},{9,10},{10,9},{11,... | collective-permute-start | bytes 786440 | tf_op jit(solution)/shard_map/ppermute | solution.py:34
  67.0 10.5 %collective-permute-start.20 = (f32[2,2,128,128]{3,2,1,0:T(8,128)S(1)}, f32[2,2,128,128]{3,2,1,0:T(8,128)S(1)}, u32[]{:S(2)}, u32[]{:S(2)}) collective-permute-start(f32[2,2,128,128]{3,2,1,0:T(8,128)S(1)} %get-tuple-element.120), channel_id=1, source_target_pairs={{0,16},{16,32},{32,48},{48,64},{64,80},{80,96},{96,112},{112,0},{1... | collective-permute-start | bytes 786440 | tf_op jit(solution)/shard_map/ppermute | solution.py:404
  71.2 7.7 %collective-permute-start.19 = (f32[256,256]{1,0:T(8,128)S(1)}, f32[256,256]{1,0:T(8,128)S(1)}, u32[]{:S(2)}, u32[]{:S(2)}) collective-permute-start(f32[256,256]{1,0:T(8,128)S(1)} %shard_map.87.e0.b0), channel_id=1, source_target_pairs={{1,2},{2,1},{3,4},{4,3},{5,6},{6,5},{7,8},{8,7},{9,10},{10,9},{11,... | collective-permute-start | bytes 786440 | tf_op jit(solution)/shard_map/ppermute | solution.py:34
  79.2 7.5 %collective-permute-start.22 = (f32[256,256]{1,0:T(8,128)S(1)}, f32[256,256]{1,0:T(8,128)S(1)}, u32[]{:S(2)}, u32[]{:S(2)}) collective-permute-start(f32[256,256]{1,0:T(8,128)S(1)} %shard_map.89.e0.b0), channel_id=1, source_target_pairs={{1,2},{2,1},{3,4},{4,3},{5,6},{6,5},{7,8},{8,7},{9,10},{10,9},{11,... | collective-permute-start | bytes 786440 | tf_op jit(solution)/shard_map/ppermute | solution.py:34
  87.0 6.9 %collective-permute-start.24 = (f32[256,256]{1,0:T(8,128)S(1)}, f32[256,256]{1,0:T(8,128)S(1)}, u32[]{:S(2)}, u32[]{:S(2)}) collective-permute-start(f32[256,256]{1,0:T(8,128)S(1)} %shard_map.91.e0.b0), channel_id=1, source_target_pairs={{1,2},{2,1},{3,4},{4,3},{5,6},{6,5},{7,8},{8,7},{9,10},{10,9},{11,... | collective-permute-start | bytes 786440 | tf_op jit(solution)/shard_map/ppermute | solution.py:34
  94.2 6.9 %collective-permute-start.26 = (f32[256,256]{1,0:T(8,128)S(1)}, f32[256,256]{1,0:T(8,128)S(1)}, u32[]{:S(2)}, u32[]{:S(2)}) collective-permute-start(f32[256,256]{1,0:T(8,128)S(1)} %shard_map.93.e0.b0), channel_id=1, source_target_pairs={{1,2},{2,1},{3,4},{4,3},{5,6},{6,5},{7,8},{8,7},{9,10},{10,9},{11,... | collective-permute-start | bytes 786440 | tf_op jit(solution)/shard_map/ppermute | solution.py:34
  101.3 6.9 %collective-permute-start.28 = (f32[256,256]{1,0:T(8,128)S(1)}, f32[256,256]{1,0:T(8,128)S(1)}, u32[]{:S(2)}, u32[]{:S(2)}) collective-permute-start(f32[256,256]{1,0:T(8,128)S(1)} %shard_map.95.e0.b0), channel_id=1, source_target_pairs={{1,2},{2,1},{3,4},{4,3},{5,6},{6,5},{7,8},{8,7},{9,10},{10,9},{11,... | collective-permute-start | bytes 786440 | tf_op jit(solution)/shard_map/ppermute | solution.py:34
  108.5 6.9 %collective-permute-start.30 = (f32[256,256]{1,0:T(8,128)S(1)}, f32[256,256]{1,0:T(8,128)S(1)}, u32[]{:S(2)}, u32[]{:S(2)}) collective-permute-start(f32[256,256]{1,0:T(8,128)S(1)} %shard_map.97.e0.b0), channel_id=1, source_target_pairs={{1,2},{2,1},{3,4},{4,3},{5,6},{6,5},{7,8},{8,7},{9,10},{10,9},{11,... | collective-permute-start | bytes 786440 | tf_op jit(solution)/shard_map/ppermute | solution.py:34
  115.6 6.9 %collective-permute-start.32 = (f32[256,256]{1,0:T(8,128)S(1)}, f32[256,256]{1,0:T(8,128)S(1)}, u32[]{:S(2)}, u32[]{:S(2)}) collective-permute-start(f32[256,256]{1,0:T(8,128)S(1)} %shard_map.99.e0.b0), channel_id=1, source_target_pairs={{1,2},{2,1},{3,4},{4,3},{5,6},{6,5},{7,8},{8,7},{9,10},{10,9},{11,... | collective-permute-start | bytes 786440 | tf_op jit(solution)/shard_map/ppermute | solution.py:34
  143.2 13.8 %collective-permute-start.34 = (f32[16,5,8,128]{3,2,1,0:T(8,128)S(1)}, f32[16,5,8,128]{3,2,1,0:T(8,128)S(1)}, u32[]{:S(2)}, u32[]{:S(2)}) collective-permute-start(f32[16,5,8,128]{3,2,1,0:T(8,128)S(1)} %slice.28.rest_0_), channel_id=1, source_target_pairs={{0,112},{16,0},{32,16},{48,32},{64,48},{80,64},{96,80},{112,96},{1... | collective-permute-start | bytes 983048 | tf_op jit(solution)/shard_map/ppermute | solution.py:450
  169.2 11.7 %collective-permute-start.39 = (f32[16,4,8,128]{3,2,1,0:T(8,128)S(1)}, f32[16,4,8,128]{3,2,1,0:T(8,128)S(1)}, u32[]{:S(2)}, u32[]{:S(2)}) collective-permute-start(f32[16,4,8,128]{3,2,1,0:T(8,128)S(1)} %shard_map.104.rest_0_), channel_id=1, source_target_pairs={{32,0},{48,16},{64,32},{80,48},{96,64},{112,80},{0,96},{16,112},{3... | collective-permute-start | bytes 786440 | tf_op jit(solution)/shard_map/ppermute | solution.py:446
  198.2 8.9 %collective-permute-start.44 = (f32[16,4,8,128]{3,2,1,0:T(8,128)S(1)}, f32[16,4,8,128]{3,2,1,0:T(8,128)S(1)}, u32[]{:S(2)}, u32[]{:S(2)}) collective-permute-start(f32[16,4,8,128]{3,2,1,0:T(8,128)S(1)} %shard_map.106), channel_id=1, source_target_pairs={{80,0},{96,16},{112,32},{0,48},{16,64},{32,80},{48,96},{64,112},{8... | collective-permute-start | bytes 786440 | tf_op jit(solution)/shard_map/ppermute | solution.py:446
  216.6 11.1 %collective-permute-start.49 = (f32[16,4,8,128]{3,2,1,0:T(8,128)S(1)}, f32[16,4,8,128]{3,2,1,0:T(8,128)S(1)}, u32[]{:S(2)}, u32[]{:S(2)}) collective-permute-start(f32[16,4,8,128]{3,2,1,0:T(8,128)S(1)} %shard_map.106), channel_id=1, source_target_pairs={{0,112},{16,0},{32,16},{48,32},{64,48},{80,64},{96,80},{112,96},{1... | collective-permute-start | bytes 786440 | tf_op jit(solution)/shard_map/ppermute | solution.py:459
  (36 other events, 161.5 us)

commit v2 on v1

--- a/solution.py
+++ b/solution.py
@@ -7,12 +7,12 @@
 from jax.experimental.pallas import tpu as pltpu
 from jax.sharding import PartitionSpec as P
 
+
 COARSE = 8
 GROUPS = 8
 SLABS = 16
 ROWS = 32
 UNROLL = 8
-HIGH = lax.Precision.HIGHEST
 
 TOUR = tuple(y * 4 + c for y in range(4) for c in (0, 1)) + tuple(
     y * 4 + 2 + c for y in reversed(range(4)) for c in (0, 1)
@@ -402,8 +402,6 @@
             )
             n1, rb, speed = lax.optimization_barrier((n1, rb, speed))
             rb = lax.ppermute(rb, "tm", ring)
-        if turn == 8:
-            n1, rb = lax.optimization_barrier((n1, rb))
         if turn < steps - 1:
             on = on_chip(n1)
         e0, inner, b0, binner = n0, ninner, e0, inner
@@ -452,7 +450,7 @@
     gradient = jnp.sum(moved[:, 4, 0, :], axis=0)[:steps]
     moved, gradient = lax.optimization_barrier((moved, gradient))
     moved = moved[:, :4] * (lax.rem(tm + GROUPS - 1, GROUPS) + 1 < GROUPS).astype(jnp.float32)
-    total = phi(moved, pieces)
+    total = phi(moved, pieces[:, :4])
     moved = later(total, 2, False)
     total = phi(phi(moved), total)
     moved = later(total, 4, True)
@@ -480,6 +478,7 @@
         P("tm"),
         P("tm", None, "space", None, None),
     )
+
     return jax.shard_map(
         body,
         mesh=mesh,

time: 259 us -> 256 us (0.988)
  transfers between devices with their start and end apart: 54 -> 54, of which waited for: 34 -> 35; matrix products, arithmetic and copies ran while one was open for 0% -> 0% of each run, Pallas kernels for 13% -> 14%
where the time goes in v2:
time: 256 us; the launch traced here: 255 us
  waiting for transfers between devices  116 us (45%)
  starting transfers between devices  58.5 us (23%)
  Pallas kernels  52.6 us (21%)
  blocking collectives  24.9 us (10%)
    ppermute x48, waiting for transfers between devices, trade(): return lax.ppermute(block, ('tm', 'space'), route)  82 us
    pallas_call x44, Pallas kernels, call(): pl.pallas_call(kernel, out_shape=out_shapes, in_specs=specs, out_specs=ja...  52.6 us
    ppermute x48, starting transfers between devices, trade(): return lax.ppermute(block, ('tm', 'space'), route)  51.1 us
    ppermute x2, waiting for transfers between devices, later(): lax.ppermute(state, 'tm', route)  20.5 us
    all_to_all x1, blocking collectives, body(): pieces = lax.all_to_all(pieces, 'space', 0, 0)  14.6 us
    all_to_all x1, blocking collectives, body(): coarse = lax.all_to_all(moved, 'space', 0, 0)  10.2 us
    ppermute x1, waiting for transfers between devices, body(): moved = lax.ppermute(pieces, 'tm', back)  7.15 us
  transfers between devices with their start and end apart: 54, of which 35 were waited for; matrix products, arithmetic and copies ran while one was open for 0% of the time, Pallas kernels for 14%

profile of v2, /device:TPU:7, one launch (start us, length us, event | category | flops | bytes accessed | tf_op | source)
XLA Modules:
  0.0 255.3 jit_solution(1457584965523362216)
XLA Ops:
  4.8 3.3 %collective-permute-start = (f32[2,16]{1,0:T(2,128)S(1)}, f32[2,16]{1,0:T(2,128)S(1)}, u32[]{:S(2)}, u32[]{:S(2)}) collective-permute-start(f32[2,16]{1,0:T(2,128)S(1)} %pad_maximum_fusion), channel_id=1, source_target_pairs={{0,16},{16,32},{32,48},{48,64},{64,80},{80,96},{96,112},{112,0},{1... | collective-permute-start | bytes 392 | tf_op jit(solution)/shard_map/ppermute | solution.py:364
  8.0 2.8 %shard_map.69 = (f32[256,256]{1,0:T(8,128)S(1)}, f32[3,256,256]{2,1,0:T(8,128)S(1)}, f32[256,256]{1,0:T(8,128)S(1)}, f32[3,256,256]{2,1,0:T(8,128)S(1)}, f32[256...) custom-call(s32[5]{0:T(128)S(1)} %stack.36.info, ...), custom_call_target="tpu_custom_call" | custom-call | tf_op jit(solution)/shard_map/pallas_call | solution.py:54
  15.4 4.2 %collective-permute-done.3.off = f32[256,256]{1,0:T(8,128)S(1)} collective-permute-done((f32[256,256]{1,0:T(8,128)S(1)}, f32[256,256]{1,0:T(8,128)S(1)}, u32[]{:S(2)}, u32[]{:S(2)}) %collective-permute-start.3) | collective-permute-done | bytes 262176 | tf_op jit(solution)/shard_map/ppermute | solution.py:34
  38.4 2.7 %collective-permute-done.9.off = f32[256,256]{1,0:T(8,128)S(1)} collective-permute-done((f32[256,256]{1,0:T(8,128)S(1)}, f32[256,256]{1,0:T(8,128)S(1)}, u32[]{:S(2)}, u32[]{:S(2)}) %collective-permute-start.9) | collective-permute-done | bytes 262176 | tf_op jit(solution)/shard_map/ppermute | solution.py:34
  45.6 2.7 %collective-permute-done.11.off = f32[256,256]{1,0:T(8,128)S(1)} collective-permute-done((f32[256,256]{1,0:T(8,128)S(1)}, f32[256,256]{1,0:T(8,128)S(1)}, u32[]{:S(2)}, u32[]{:S(2)}) %collective-permute-start.11) | collective-permute-done | bytes 262176 | tf_op jit(solution)/shard_map/ppermute | solution.py:34
  52.7 2.7 %collective-permute-done.13.off = f32[256,256]{1,0:T(8,128)S(1)} collective-permute-done((f32[256,256]{1,0:T(8,128)S(1)}, f32[256,256]{1,0:T(8,128)S(1)}, u32[]{:S(2)}, u32[]{:S(2)}) %collective-permute-start.13) | collective-permute-done | bytes 262176 | tf_op jit(solution)/shard_map/ppermute | solution.py:34
  59.9 2.7 %collective-permute-done.15.off = f32[256,256]{1,0:T(8,128)S(1)} collective-permute-done((f32[256,256]{1,0:T(8,128)S(1)}, f32[256,256]{1,0:T(8,128)S(1)}, u32[]{:S(2)}, u32[]{:S(2)}) %collective-permute-start.15) | collective-permute-done | bytes 262176 | tf_op jit(solution)/shard_map/ppermute | solution.py:34
  67.0 2.7 %collective-permute-done.17.off = f32[256,256]{1,0:T(8,128)S(1)} collective-permute-done((f32[256,256]{1,0:T(8,128)S(1)}, f32[256,256]{1,0:T(8,128)S(1)}, u32[]{:S(2)}, u32[]{:S(2)}) %collective-permute-start.17) | collective-permute-done | bytes 262176 | tf_op jit(solution)/shard_map/ppermute | solution.py:34
  117.2 3.9 %collective-permute-start.33 = (f32[2,2,128,128]{3,2,1,0:T(8,128)S(1)}, f32[2,2,128,128]{3,2,1,0:T(8,128)S(1)}, u32[]{:S(2)}, u32[]{:S(2)}) collective-permute-start(f32[2,2,128,128]{3,2,1,0:T(8,128)S(1)} %get-tuple-element.139), channel_id=1, source_target_pairs={{0,16},{16,32},{32,48},{48,64},{64,80},{80,96},{96,112},{112,0},{1... | collective-permute-start | bytes 786440 | tf_op jit(solution)/shard_map/ppermute | solution.py:404
  123.6 2.7 %collective-permute-done.33.rb = f32[2,2,128,128]{3,2,1,0:T(8,128)S(1)} collective-permute-done((f32[2,2,128,128]{3,2,1,0:T(8,128)S(1)}, f32[2,2,128,128]{3,2,1,0:T(8,128)S(1)}, u32[]{:S(2)}, u32[]{:S(2)}) %collective-permute-start.33) | collective-permute-done | bytes 262176 | tf_op jit(solution)/shard_map/ppermute | solution.py:404
  127.5 14.6 %all_to_all.10 = f32[16,7,8,128]{3,2,1,0:T(8,128)S(1)} all-to-all(f32[16,7,8,128]{3,2,1,0:T(8,128)S(1)} %shard_map.103), channel_id=1, replica_groups=mesh['tm'=8,'space'=16] {'space'}, dimensions={0} | all-to-all | bytes 917504 | tf_op jit(solution)/shard_map/all_to_all | solution.py:416
  145.0 3.7 %collective-permute-done.36.soff = f32[16,2,8,128]{3,2,1,0:T(8,128)S(1)} collective-permute-done((f32[16,2,8,128]{3,2,1,0:T(8,128)S(1)}, f32[16,2,8,128]{3,2,1,0:T(8,128)S(1)}, u32[]{:S(2)}, u32[]{:S(2)}) %collective-permute-start.36) | collective-permute-done | bytes 131104 | tf_op jit(solution)/shard_map/ppermute | solution.py:34
  148.7 7.2 %collective-permute-done.34 = f32[16,5,8,128]{3,2,1,0:T(8,128)S(1)} collective-permute-done((f32[16,5,8,128]{3,2,1,0:T(8,128)S(1)}, f32[16,5,8,128]{3,2,1,0:T(8,128)S(1)}, u32[]{:S(2)}, u32[]{:S(2)}) %collective-permute-start.34) | collective-permute-done | bytes 327712 | tf_op jit(solution)/shard_map/ppermute | solution.py:448
  159.3 4.6 %collective-permute-done.38.off = f32[16,4,8,128]{3,2,1,0:T(8,128)S(1)} collective-permute-done((f32[16,4,8,128]{3,2,1,0:T(8,128)S(1)}, f32[16,4,8,128]{3,2,1,0:T(8,128)S(1)}, u32[]{:S(2)}, u32[]{:S(2)}) %collective-permute-start.38) | collective-permute-done | bytes 262176 | tf_op jit(solution)/shard_map/ppermute | solution.py:34
  166.1 11.7 %collective-permute-done.39 = f32[16,4,8,128]{3,2,1,0:T(8,128)S(1)} collective-permute-done((f32[16,4,8,128]{3,2,1,0:T(8,128)S(1)}, f32[16,4,8,128]{3,2,1,0:T(8,128)S(1)}, u32[]{:S(2)}, u32[]{:S(2)}) %collective-permute-start.39) | collective-permute-done | bytes 262176 | tf_op jit(solution)/shard_map/ppermute | solution.py:444
  180.0 4.6 %collective-permute-done.41.off = f32[16,4,8,128]{3,2,1,0:T(8,128)S(1)} collective-permute-done((f32[16,4,8,128]{3,2,1,0:T(8,128)S(1)}, f32[16,4,8,128]{3,2,1,0:T(8,128)S(1)}, u32[]{:S(2)}, u32[]{:S(2)}) %collective-permute-start.41) | collective-permute-done | bytes 262176 | tf_op jit(solution)/shard_map/ppermute | solution.py:34
  188.3 4.6 %collective-permute-done.43.off = f32[16,4,8,128]{3,2,1,0:T(8,128)S(1)} collective-permute-done((f32[16,4,8,128]{3,2,1,0:T(8,128)S(1)}, f32[16,4,8,128]{3,2,1,0:T(8,128)S(1)}, u32[]{:S(2)}, u32[]{:S(2)}) %collective-permute-start.43) | collective-permute-done | bytes 262176 | tf_op jit(solution)/shard_map/ppermute | solution.py:34
  195.1 8.9 %collective-permute-done.44 = f32[16,4,8,128]{3,2,1,0:T(8,128)S(1)} collective-permute-done((f32[16,4,8,128]{3,2,1,0:T(8,128)S(1)}, f32[16,4,8,128]{3,2,1,0:T(8,128)S(1)}, u32[]{:S(2)}, u32[]{:S(2)}) %collective-permute-start.44) | collective-permute-done | bytes 262176 | tf_op jit(solution)/shard_map/ppermute | solution.py:444
  206.3 4.6 %collective-permute-done.46.off = f32[16,4,8,128]{3,2,1,0:T(8,128)S(1)} collective-permute-done((f32[16,4,8,128]{3,2,1,0:T(8,128)S(1)}, f32[16,4,8,128]{3,2,1,0:T(8,128)S(1)}, u32[]{:S(2)}, u32[]{:S(2)}) %collective-permute-start.46) | collective-permute-done | bytes 262176 | tf_op jit(solution)/shard_map/ppermute | solution.py:34
  214.6 4.6 %collective-permute-done.48.off = f32[16,4,8,128]{3,2,1,0:T(8,128)S(1)} collective-permute-done((f32[16,4,8,128]{3,2,1,0:T(8,128)S(1)}, f32[16,4,8,128]{3,2,1,0:T(8,128)S(1)}, u32[]{:S(2)}, u32[]{:S(2)}) %collective-permute-start.48) | collective-permute-done | bytes 262176 | tf_op jit(solution)/shard_map/ppermute | solution.py:34
  221.3 3.2 %collective-permute-done.49.rest_0_ = f32[16,4,8,128]{3,2,1,0:T(8,128)S(1)} collective-permute-done((f32[16,4,8,128]{3,2,1,0:T(8,128)S(1)}, f32[16,4,8,128]{3,2,1,0:T(8,128)S(1)}, u32[]{:S(2)}, u32[]{:S(2)}) %collective-permute-start.49) | collective-permute-done | bytes 262176 | tf_op jit(solution)/shard_map/ppermute | solution.py:457
  228.3 4.6 %collective-permute-done.51.off = f32[16,4,8,128]{3,2,1,0:T(8,128)S(1)} collective-permute-done((f32[16,4,8,128]{3,2,1,0:T(8,128)S(1)}, f32[16,4,8,128]{3,2,1,0:T(8,128)S(1)}, u32[]{:S(2)}, u32[]{:S(2)}) %collective-permute-start.51) | collective-permute-done | bytes 262176 | tf_op jit(solution)/shard_map/ppermute | solution.py:34
  236.7 4.4 %collective-permute-done.53.off = f32[16,4,8,128]{3,2,1,0:T(8,128)S(1)} collective-permute-done((f32[16,4,8,128]{3,2,1,0:T(8,128)S(1)}, f32[16,4,8,128]{3,2,1,0:T(8,128)S(1)}, u32[]{:S(2)}, u32[]{:S(2)}) %collective-permute-start.53) | collective-permute-done | bytes 262176 | tf_op jit(solution)/shard_map/ppermute | solution.py:34
  243.1 10.2 %all_to_all.11.coarse = f32[16,4,8,128]{3,2,1,0:T(8,128)S(1)} all-to-all(f32[16,4,8,128]{3,2,1,0:T(8,128)S(1)} %shard_map.110), channel_id=1, replica_groups=mesh['tm'=8,'space'=16] {'space'}, dimensions={0} | all-to-all | bytes 524288 | tf_op jit(solution)/shard_map/all_to_all | solution.py:462
  (156 shorter events, 132.2 us)
Async XLA Ops:
  2.4 11.4 %collective-permute-start.2 = (f32[256,256]{1,0:T(8,128)S(1)}, f32[256,256]{1,0:T(8,128)S(1)}, u32[]{:S(2)}, u32[]{:S(2)}) collective-permute-start(f32[256,256]{1,0:T(8,128)S(1)} %get-tuple-element.84), channel_id=1, source_target_pairs={{0,1},{1,0},{2,3},{3,2},{4,5},{5,4},{6,7},{7,6},{8,9},{9,8},{10,11... | collective-permute-start | bytes 786440 | tf_op jit(solution)/shard_map/ppermute | solution.py:34
  3.1 7.8 %collective-permute-start.1 = (f32[256,256]{1,0:T(8,128)S(1)}, f32[256,256]{1,0:T(8,128)S(1)}, u32[]{:S(2)}, u32[]{:S(2)}) collective-permute-start(f32[256,256]{1,0:T(8,128)S(1)} %get-tuple-element.75), channel_id=1, source_target_pairs={{1,2},{2,1},{3,4},{4,3},{5,6},{6,5},{7,8},{8,7},{9,10},{10,9},{11,... | collective-permute-start | bytes 786440 | tf_op jit(solution)/shard_map/ppermute | solution.py:34
  11.3 8.3 %collective-permute-start.3 = (f32[256,256]{1,0:T(8,128)S(1)}, f32[256,256]{1,0:T(8,128)S(1)}, u32[]{:S(2)}, u32[]{:S(2)}) collective-permute-start(f32[256,256]{1,0:T(8,128)S(1)} %shard_map.70.e0.b0), channel_id=1, source_target_pairs={{1,2},{2,1},{3,4},{4,3},{5,6},{6,5},{7,8},{8,7},{9,10},{10,9},{11,... | collective-permute-start | bytes 786440 | tf_op jit(solution)/shard_map/ppermute | solution.py:34
  15.3 7.1 %collective-permute-start.4 = (f32[256,256]{1,0:T(8,128)S(1)}, f32[256,256]{1,0:T(8,128)S(1)}, u32[]{:S(2)}, u32[]{:S(2)}) collective-permute-start(f32[256,256]{1,0:T(8,128)S(1)} %get-tuple-element.88), channel_id=1, source_target_pairs={{0,1},{1,0},{2,3},{3,2},{4,5},{5,4},{6,7},{7,6},{8,9},{9,8},{10,11... | collective-permute-start | bytes 786440 | tf_op jit(solution)/shard_map/ppermute | solution.py:34
  19.9 6.9 %collective-permute-start.5 = (f32[256,256]{1,0:T(8,128)S(1)}, f32[256,256]{1,0:T(8,128)S(1)}, u32[]{:S(2)}, u32[]{:S(2)}) collective-permute-start(f32[256,256]{1,0:T(8,128)S(1)} %shard_map.72.e0.b0), channel_id=1, source_target_pairs={{1,2},{2,1},{3,4},{4,3},{5,6},{6,5},{7,8},{8,7},{9,10},{10,9},{11,... | collective-permute-start | bytes 786440 | tf_op jit(solution)/shard_map/ppermute | solution.py:34
  24.0 6.6 %collective-permute-start.6 = (f32[256,256]{1,0:T(8,128)S(1)}, f32[256,256]{1,0:T(8,128)S(1)}, u32[]{:S(2)}, u32[]{:S(2)}) collective-permute-start(f32[256,256]{1,0:T(8,128)S(1)} %get-tuple-element.91), channel_id=1, source_target_pairs={{0,1},{1,0},{2,3},{3,2},{4,5},{5,4},{6,7},{7,6},{8,9},{9,8},{10,11... | collective-permute-start | bytes 786440 | tf_op jit(solution)/shard_map/ppermute | solution.py:34
  27.0 6.9 %collective-permute-start.7 = (f32[256,256]{1,0:T(8,128)S(1)}, f32[256,256]{1,0:T(8,128)S(1)}, u32[]{:S(2)}, u32[]{:S(2)}) collective-permute-start(f32[256,256]{1,0:T(8,128)S(1)} %shard_map.74.e0.b0), channel_id=1, source_target_pairs={{1,2},{2,1},{3,4},{4,3},{5,6},{6,5},{7,8},{8,7},{9,10},{10,9},{11,... | collective-permute-start | bytes 786440 | tf_op jit(solution)/shard_map/ppermute | solution.py:34
  34.2 6.9 %collective-permute-start.9 = (f32[256,256]{1,0:T(8,128)S(1)}, f32[256,256]{1,0:T(8,128)S(1)}, u32[]{:S(2)}, u32[]{:S(2)}) collective-permute-start(f32[256,256]{1,0:T(8,128)S(1)} %shard_map.76.e0.b0), channel_id=1, source_target_pairs={{1,2},{2,1},{3,4},{4,3},{5,6},{6,5},{7,8},{8,7},{9,10},{10,9},{11,... | collective-permute-start | bytes 786440 | tf_op jit(solution)/shard_map/ppermute | solution.py:34
  41.4 6.9 %collective-permute-start.11 = (f32[256,256]{1,0:T(8,128)S(1)}, f32[256,256]{1,0:T(8,128)S(1)}, u32[]{:S(2)}, u32[]{:S(2)}) collective-permute-start(f32[256,256]{1,0:T(8,128)S(1)} %shard_map.79.e0.b0), channel_id=1, source_target_pairs={{1,2},{2,1},{3,4},{4,3},{5,6},{6,5},{7,8},{8,7},{9,10},{10,9},{11,... | collective-permute-start | bytes 786440 | tf_op jit(solution)/shard_map/ppermute | solution.py:34
  48.5 6.9 %collective-permute-start.13 = (f32[256,256]{1,0:T(8,128)S(1)}, f32[256,256]{1,0:T(8,128)S(1)}, u32[]{:S(2)}, u32[]{:S(2)}) collective-permute-start(f32[256,256]{1,0:T(8,128)S(1)} %shard_map.81.e0.b0), channel_id=1, source_target_pairs={{1,2},{2,1},{3,4},{4,3},{5,6},{6,5},{7,8},{8,7},{9,10},{10,9},{11,... | collective-permute-start | bytes 786440 | tf_op jit(solution)/shard_map/ppermute | solution.py:34
  55.7 6.9 %collective-permute-start.15 = (f32[256,256]{1,0:T(8,128)S(1)}, f32[256,256]{1,0:T(8,128)S(1)}, u32[]{:S(2)}, u32[]{:S(2)}) collective-permute-start(f32[256,256]{1,0:T(8,128)S(1)} %shard_map.83.e0.b0), channel_id=1, source_target_pairs={{1,2},{2,1},{3,4},{4,3},{5,6},{6,5},{7,8},{8,7},{9,10},{10,9},{11,... | collective-permute-start | bytes 786440 | tf_op jit(solution)/shard_map/ppermute | solution.py:34
  62.8 6.9 %collective-permute-start.17 = (f32[256,256]{1,0:T(8,128)S(1)}, f32[256,256]{1,0:T(8,128)S(1)}, u32[]{:S(2)}, u32[]{:S(2)}) collective-permute-start(f32[256,256]{1,0:T(8,128)S(1)} %shard_map.85.e0.b0), channel_id=1, source_target_pairs={{1,2},{2,1},{3,4},{4,3},{5,6},{6,5},{7,8},{8,7},{9,10},{10,9},{11,... | collective-permute-start | bytes 786440 | tf_op jit(solution)/shard_map/ppermute | solution.py:34
  70.0 6.9 %collective-permute-start.19 = (f32[256,256]{1,0:T(8,128)S(1)}, f32[256,256]{1,0:T(8,128)S(1)}, u32[]{:S(2)}, u32[]{:S(2)}) collective-permute-start(f32[256,256]{1,0:T(8,128)S(1)} %shard_map.87.e0.b0), channel_id=1, source_target_pairs={{1,2},{2,1},{3,4},{4,3},{5,6},{6,5},{7,8},{8,7},{9,10},{10,9},{11,... | collective-permute-start | bytes 786440 | tf_op jit(solution)/shard_map/ppermute | solution.py:34
  77.2 6.9 %collective-permute-start.21 = (f32[256,256]{1,0:T(8,128)S(1)}, f32[256,256]{1,0:T(8,128)S(1)}, u32[]{:S(2)}, u32[]{:S(2)}) collective-permute-start(f32[256,256]{1,0:T(8,128)S(1)} %shard_map.89.e0.b0), channel_id=1, source_target_pairs={{1,2},{2,1},{3,4},{4,3},{5,6},{6,5},{7,8},{8,7},{9,10},{10,9},{11,... | collective-permute-start | bytes 786440 | tf_op jit(solution)/shard_map/ppermute | solution.py:34
  84.3 6.9 %collective-permute-start.23 = (f32[256,256]{1,0:T(8,128)S(1)}, f32[256,256]{1,0:T(8,128)S(1)}, u32[]{:S(2)}, u32[]{:S(2)}) collective-permute-start(f32[256,256]{1,0:T(8,128)S(1)} %shard_map.91.e0.b0), channel_id=1, source_target_pairs={{1,2},{2,1},{3,4},{4,3},{5,6},{6,5},{7,8},{8,7},{9,10},{10,9},{11,... | collective-permute-start | bytes 786440 | tf_op jit(solution)/shard_map/ppermute | solution.py:34
  91.5 6.9 %collective-permute-start.25 = (f32[256,256]{1,0:T(8,128)S(1)}, f32[256,256]{1,0:T(8,128)S(1)}, u32[]{:S(2)}, u32[]{:S(2)}) collective-permute-start(f32[256,256]{1,0:T(8,128)S(1)} %shard_map.93.e0.b0), channel_id=1, source_target_pairs={{1,2},{2,1},{3,4},{4,3},{5,6},{6,5},{7,8},{8,7},{9,10},{10,9},{11,... | collective-permute-start | bytes 786440 | tf_op jit(solution)/shard_map/ppermute | solution.py:34
  98.7 6.9 %collective-permute-start.27 = (f32[256,256]{1,0:T(8,128)S(1)}, f32[256,256]{1,0:T(8,128)S(1)}, u32[]{:S(2)}, u32[]{:S(2)}) collective-permute-start(f32[256,256]{1,0:T(8,128)S(1)} %shard_map.95.e0.b0), channel_id=1, source_target_pairs={{1,2},{2,1},{3,4},{4,3},{5,6},{6,5},{7,8},{8,7},{9,10},{10,9},{11,... | collective-permute-start | bytes 786440 | tf_op jit(solution)/shard_map/ppermute | solution.py:34
  105.8 6.9 %collective-permute-start.29 = (f32[256,256]{1,0:T(8,128)S(1)}, f32[256,256]{1,0:T(8,128)S(1)}, u32[]{:S(2)}, u32[]{:S(2)}) collective-permute-start(f32[256,256]{1,0:T(8,128)S(1)} %shard_map.97.e0.b0), channel_id=1, source_target_pairs={{1,2},{2,1},{3,4},{4,3},{5,6},{6,5},{7,8},{8,7},{9,10},{10,9},{11,... | collective-permute-start | bytes 786440 | tf_op jit(solution)/shard_map/ppermute | solution.py:34
  113.0 8.1 %collective-permute-start.31 = (f32[256,256]{1,0:T(8,128)S(1)}, f32[256,256]{1,0:T(8,128)S(1)}, u32[]{:S(2)}, u32[]{:S(2)}) collective-permute-start(f32[256,256]{1,0:T(8,128)S(1)} %shard_map.99.e0.b0), channel_id=1, source_target_pairs={{1,2},{2,1},{3,4},{4,3},{5,6},{6,5},{7,8},{8,7},{9,10},{10,9},{11,... | collective-permute-start | bytes 786440 | tf_op jit(solution)/shard_map/ppermute | solution.py:34
  117.2 9.1 %collective-permute-start.33 = (f32[2,2,128,128]{3,2,1,0:T(8,128)S(1)}, f32[2,2,128,128]{3,2,1,0:T(8,128)S(1)}, u32[]{:S(2)}, u32[]{:S(2)}) collective-permute-start(f32[2,2,128,128]{3,2,1,0:T(8,128)S(1)} %get-tuple-element.139), channel_id=1, source_target_pairs={{0,16},{16,32},{32,48},{48,64},{64,80},{80,96},{96,112},{112,0},{1... | collective-permute-start | bytes 786440 | tf_op jit(solution)/shard_map/ppermute | solution.py:404
  142.2 13.6 %collective-permute-start.34 = (f32[16,5,8,128]{3,2,1,0:T(8,128)S(1)}, f32[16,5,8,128]{3,2,1,0:T(8,128)S(1)}, u32[]{:S(2)}, u32[]{:S(2)}) collective-permute-start(f32[16,5,8,128]{3,2,1,0:T(8,128)S(1)} %slice.33), channel_id=1, source_target_pairs={{0,112},{16,0},{32,16},{48,32},{64,48},{80,64},{96,80},{112,96},{1... | collective-permute-start | bytes 983048 | tf_op jit(solution)/shard_map/ppermute | solution.py:448
  166.1 11.7 %collective-permute-start.39 = (f32[16,4,8,128]{3,2,1,0:T(8,128)S(1)}, f32[16,4,8,128]{3,2,1,0:T(8,128)S(1)}, u32[]{:S(2)}, u32[]{:S(2)}) collective-permute-start(f32[16,4,8,128]{3,2,1,0:T(8,128)S(1)} %shard_map.104.rest_0_), channel_id=1, source_target_pairs={{32,0},{48,16},{64,32},{80,48},{96,64},{112,80},{0,96},{16,112},{3... | collective-permute-start | bytes 786440 | tf_op jit(solution)/shard_map/ppermute | solution.py:444
  195.0 8.9 %collective-permute-start.44 = (f32[16,4,8,128]{3,2,1,0:T(8,128)S(1)}, f32[16,4,8,128]{3,2,1,0:T(8,128)S(1)}, u32[]{:S(2)}, u32[]{:S(2)}) collective-permute-start(f32[16,4,8,128]{3,2,1,0:T(8,128)S(1)} %shard_map.106), channel_id=1, source_target_pairs={{80,0},{96,16},{112,32},{0,48},{16,64},{32,80},{48,96},{64,112},{8... | collective-permute-start | bytes 786440 | tf_op jit(solution)/shard_map/ppermute | solution.py:444
  213.5 11.1 %collective-permute-start.49 = (f32[16,4,8,128]{3,2,1,0:T(8,128)S(1)}, f32[16,4,8,128]{3,2,1,0:T(8,128)S(1)}, u32[]{:S(2)}, u32[]{:S(2)}) collective-permute-start(f32[16,4,8,128]{3,2,1,0:T(8,128)S(1)} %shard_map.106), channel_id=1, source_target_pairs={{0,112},{16,0},{32,16},{48,32},{64,48},{80,64},{96,80},{112,96},{1... | collective-permute-start | bytes 786440 | tf_op jit(solution)/shard_map/ppermute | solution.py:457
  (35 other events, 162.4 us)
